TPU v7x, 128 devices: a whole 4x4x4 slice. The times are simulated.
128 devices in a mesh: row: 16 (over y, x), col: 8 (over z, core).
Axes of the slice: x: 4, y: 4, z: 4, core: 2. Of those that a mesh axis runs over, the one named last changes fastest.
Arguments:
- samples: bfloat16 [16384, 768], P(('row', 'col')), may hold values from -8 to 8, as said below
Outputs:
- factored: float32 [16384, 16384], P('row', 'col')
Inputs may be any that keep to these rules, and one draw needn't show every extreme that they name: `samples`: every entry is a feature value.
All inputs are finite; a program needn't handle non-finite values.
Results may differ from a plain program's by a relative error of at most 0.0003.
Values may be sent and summed in bfloat16 or wider, within the bound.
No kernel may reach another device: no remote copies, remote signals or barrier semaphores. Data moves between devices by JAX's collectives and lax.ppermute only.
A program may use at most 128 MiB of HBM per device.

v0:
```python
import math

import jax
import jax.numpy as jnp
from jax import lax
from jax.sharding import PartitionSpec as P

FEAT = 768
PANEL = 512
LAYERS = 8


def broadcast(block, axis, owner):
    block = jnp.where(lax.axis_index(axis) == owner, block, jnp.zeros_like(block))
    return lax.psum(block, axis)


def ntk_tile(left_rows, right_rows, row_ids, col_ids):
    gram_tile = (
        lax.dot_general(
            left_rows, right_rows, (((1,), (1,)), ((), ())), preferred_element_type=jnp.float32
        )
        / FEAT
    )
    left_f = left_rows.astype(jnp.float32)
    right_f = right_rows.astype(jnp.float32)
    row_norms = jnp.sum(left_f * left_f, axis=1) / FEAT
    col_norms = jnp.sum(right_f * right_f, axis=1) / FEAT
    on_diag = row_ids[:, None] == col_ids[None, :]
    norm_scale = jnp.sqrt(row_norms[:, None] * col_norms[None, :])
    covariance = gram_tile
    tangent = gram_tile
    for layer_step in range(LAYERS):
        cosine = jnp.where(on_diag, jnp.float32(1.0), covariance / norm_scale)
        angles = jnp.arccos(cosine)
        sine_part = jnp.sqrt(jnp.maximum(1.0 - cosine * cosine, 0.0))
        covariance = norm_scale / math.pi * (sine_part + (math.pi - angles) * cosine)
        tangent = covariance + tangent * (1.0 - angles / math.pi)
    return tangent / (LAYERS + 1.0) + jnp.where(on_diag, jnp.float32(1.0), jnp.float32(0.0))


def per_device(samples):
    row_count = lax.axis_size("row")
    col_count = lax.axis_size("col")
    share_count = row_count // col_count
    row_index = lax.axis_index("row")
    col_index = lax.axis_index("col")
    row_block = PANEL // row_count
    col_block = PANEL // col_count
    row_feats = lax.all_gather(samples, "col", axis=0, tiled=True)
    rows_dev = row_feats.shape[0]
    feat_count = row_feats.shape[1]
    blocks = rows_dev // row_block
    cols_dev = rows_dev * share_count
    every_row = lax.all_gather(row_feats, "row", axis=0, tiled=True)
    grouped = every_row.reshape(col_count, share_count, blocks, row_block, feat_count)
    own_group = lax.dynamic_index_in_dim(grouped, col_index, 0, keepdims=False)
    col_feats = jnp.swapaxes(own_group, 0, 1).reshape(cols_dev, feat_count)
    local_rows = jnp.arange(rows_dev, dtype=jnp.int32)
    row_ids = local_rows // row_block * PANEL + row_index * row_block + local_rows % row_block
    local_cols = jnp.arange(cols_dev, dtype=jnp.int32)
    col_ids = local_cols // col_block * PANEL + col_index * col_block + local_cols % col_block
    kernel = ntk_tile(row_feats, col_feats, row_ids, col_ids)
    panel_cols = lax.all_gather(kernel[:, :col_block], "col", axis=1, tiled=True)
    corner = lax.all_gather(panel_cols[:row_block], "row", axis=0, tiled=True)
    corner_factor = jnp.linalg.cholesky(corner)
    solved = lax.linalg.triangular_solve(
        corner_factor, panel_cols, left_side=False, lower=True, transpose_a=True
    )
    top_rows = lax.dynamic_slice_in_dim(corner_factor, row_index * row_block, row_block, 0)
    panel_row = jnp.concatenate([top_rows, solved[row_block:]], axis=0)
    sections = []
    for member in range(share_count):
        received = broadcast(panel_row, "row", col_index * share_count + member)
        sections.append(received.reshape(blocks, row_block, PANEL))
    panel_col = jnp.stack(sections, axis=1).reshape(cols_dev, PANEL)
    update = kernel[:, col_block:] - lax.dot_general(
        panel_row,
        panel_col[col_block:],
        (((1,), (1,)), ((), ())),
        precision=lax.Precision.HIGHEST,
        preferred_element_type=jnp.float32,
    )
    left_part = lax.dynamic_slice_in_dim(panel_row, col_index * col_block, col_block, 1)
    result = jnp.concatenate([left_part, update], axis=1)
    return jnp.where(row_ids[:, None] >= col_ids[None, :], result, jnp.float32(0.0))


def solution(mesh):
    return jax.shard_map(
        per_device,
        mesh=mesh,
        in_specs=(P(("row", "col"), None),),
        out_specs=P("row", "col"),
        check_vma=False,
    )
```

profile of v0, /device:TPU:1, one launch (start us, length us, event | category | flops | bytes accessed | tf_op | source)
XLA Modules:
  0.0 820.3 jit_solution(1117322185920073953)
XLA Ops:
  7.3 30.0 %all-gather.5.cloned.1.call-done = bf16[1024,768]{1,0:T(8,128)(2,1)} async-done(((bf16[128,768]{1,0:T(8,128)(2,1)}), bf16[1024,768]{1,0:T(8,128)(2,1)}) %all-gather.5.cloned.1.call-update) | async-done | bytes 1572880 | tf_op jit(solution)/shard_map/all_gather | solution.py:50
  39.3 153.4 %all-gather.7.cloned.1.call-done = bf16[16384,768]{1,0:T(8,128)(2,1)} async-done(((bf16[1024,768]{1,0:T(8,128)(2,1)}), bf16[16384,768]{1,0:T(8,128)(2,1)}) %all-gather.7.cloned.1.call-update) | async-done | bytes 25165840 | tf_op jit(solution)/shard_map/all_gather | solution.py:55
  192.7 2.6 multiply_reduce_fusion
  199.5 251.8 %fusion = f32[1024,2048]{0,1:T(8,128)S(1)} fusion(bf16[2048,768]{1,0:T(8,128)(2,1)} %bitcast.106, bf16[1024,768]{1,0:T(8,128)(2,1)S(1)} %copy-done.1, f32[2048]{0:T(1024)S(1)} %div.118, f32[1024]{0:T(1024)S(1)} %broadcast_multiply_fusion.1, s32[1024]{0:T(1024)S(1)} %fusion.75, s32[2048]{0:T(1024)S(1)} %fusion.65), kind=kOutput, calls=%fused_computation.11 | convolution fusion | flops 3504340992 | bytes 13131776 | tf_op jit(solution)/shard_map/dot_general | solution.py:20
  451.3 3.4 copy-done
  455.5 25.9 %all-gather.9.cloned.1.call-done = f32[1024,512]{0,1:T(8,128)} async-done(((f32[1024,64]{0,1:T(8,128)}), f32[1024,512]{0,1:T(8,128)}) %all-gather.9.cloned.1.call-update) | async-done | bytes 2097168 | tf_op jit(solution)/shard_map/all_gather | solution.py:64
  483.2 40.6 %all-gather.11.cloned.1.call-done = f32[512,512]{1,0:T(8,128)} async-done(((f32[32,512]{1,0:T(8,128)}), f32[512,512]{1,0:T(8,128)}) %all-gather.11.cloned.1.call-update) | async-done | bytes 1048592 | tf_op jit(solution)/shard_map/all_gather | solution.py:65
  526.8 11.7 %cholesky.104 = f32[128,128]{1,0:T(8,128)S(1)} custom-call(f32[128,128]{1,0:T(8,128)S(1)} %cholesky.266), custom_call_target="Cholesky" | custom-call | tf_op jit(solution)/shard_map/jit(cholesky)/cholesky | solution.py:66
  538.6 9.8 %custom-call.30 = f32[1,128,128]{1,2,0:T(8,128)S(1)} custom-call(f32[1,128,128]{2,1,0:T(8,128)S(1)} %get-tuple-element.46), custom_call_target="InvertDiagBlocksLowerTriangular" | custom-call | tf_op jit(solution)/shard_map/jit(cholesky)/cholesky | solution.py:66
  549.2 11.7 %cholesky.217 = f32[128,128]{1,0:T(8,128)S(1)} custom-call(f32[128,128]{1,0:T(8,128)S(1)} %cholesky.270), custom_call_target="Cholesky" | custom-call | tf_op jit(solution)/shard_map/jit(cholesky)/cholesky | solution.py:66
  560.9 10.0 %custom-call.31 = f32[1,128,128]{1,2,0:T(8,128)S(1)} custom-call(f32[1,128,128]{2,1,0:T(8,128)S(1)} %get-tuple-element.43), custom_call_target="InvertDiagBlocksLowerTriangular" | custom-call | tf_op jit(solution)/shard_map/jit(cholesky)/cholesky | solution.py:66
  571.6 11.7 %cholesky.238 = f32[128,128]{1,0:T(8,128)S(1)} custom-call(f32[128,128]{1,0:T(8,128)S(1)} %cholesky.275), custom_call_target="Cholesky" | custom-call | tf_op jit(solution)/shard_map/jit(cholesky)/cholesky | solution.py:66
  584.0 9.8 %custom-call.32 = f32[1,128,128]{1,2,0:T(8,128)S(1)} custom-call(f32[1,128,128]{2,1,0:T(8,128)S(1)} %get-tuple-element.40), custom_call_target="InvertDiagBlocksLowerTriangular" | custom-call | tf_op jit(solution)/shard_map/jit(cholesky)/cholesky | solution.py:66
  594.4 11.7 %cholesky.255 = f32[128,128]{1,0:T(8,128)S(1)} custom-call(f32[128,128]{1,0:T(8,128)S(1)} %convolution_subtract_fusion.4), custom_call_target="Cholesky" | custom-call | tf_op jit(solution)/shard_map/jit(cholesky)/cholesky | solution.py:66
  610.5 7.8 while.1
  618.4 39.3 %custom-call.33 = f32[4,128,128]{1,2,0:T(8,128)S(1)} custom-call(f32[4,128,128]{2,1,0:T(8,128)S(1)} %get-tuple-element.12), custom_call_target="InvertDiagBlocksLowerTriangular" | custom-call | tf_op jit(solution)/shard_map/triangular_solve | solution.py:67
  664.2 2.2 fusion.30
  668.8 2.9 copy.33
  673.3 2.9 copy.34
  676.2 104.3 %all-reduce.4.cloned.1.call-done = (f32[32,1,32,512]{3,2,0,1:T(8,128)}, f32[32,1,32,512]{3,2,0,1:T(8,128)}) async-done(((f32[32,1,32,512]{3,2,0,1:T(8,128)}, f32[32,1,32,512]{3,2,0,1:T(8,128)}), (f32[32,1,32,512]{3,2,0,1:T(8,128)}, f32[32,1,32,512]{3,2,0,1:T(8,128)})) %all-reduce.4.cloned.1.call-update) | async-done | bytes 4194320 | tf_op jit(solution)/shard_map/psum | solution.py:15
  780.5 2.7 pad_maximum_fusion
  784.0 16.9 %slice_subtract_fusion = f32[1024,1984]{0,1:T(8,128)S(1)} fusion(f32[1024,2048]{0,1:T(8,128)} %copy-done, f32[1024,512]{0,1:T(8,128)S(1)} %get-tuple-element.32, f32[1984,512]{1,0:T(8,128)S(1)} %bitcast.103), kind=kOutput, calls=%fused_computation.43 | convolution fusion | flops 12484280320 | bytes 22413312 | tf_op jit(solution)/shard_map/dot_general | solution.py:77
  800.8 3.6 maximum_select_fusion
  804.4 9.1 %copy.36 = f32[1024,2048]{1,0:T(8,128)} copy(f32[1024,2048]{0,1:T(8,128)} %maximum_select_fusion) | data formatting | bytes 16777216 | tf_op jit(solution)/shard_map/jit(_where)/select_n | solution.py:86
  (71 shorter events, 36.1 us)
Async XLA Ops:
  6.5 30.8 %all-gather.5.cloned.1.call-start = ((), (), s32[]{:S(2)}) async-start(), calls=%async_computation | async-start | bytes 1769472 | tf_op jit(solution)/shard_map/all_gather | solution.py:50
  7.3 185.5 %all-gather.7.cloned.1.call-start = ((), (), s32[]{:S(2)}) async-start(), calls=%async_computation.1 | async-start | bytes 26738688 | tf_op jit(solution)/shard_map/all_gather | solution.py:55
  37.3 444.1 %all-gather.9.cloned.1.call-start = ((), (), s32[]{:S(2)}) async-start(), calls=%async_computation.2 | async-start | bytes 2359296 | tf_op jit(solution)/shard_map/all_gather | solution.py:64
  37.4 162.1 %copy-start.1 = (bf16[1024,768]{1,0:T(8,128)(2,1)S(1)}, bf16[1024,768]{1,0:T(8,128)(2,1)}, u32[]{:S(2)}) copy-start(bf16[1024,768]{1,0:T(8,128)(2,1)} %all-gather.5.cloned.1.call-done) | copy-start | bytes 4718596
  451.3 3.4 copy-start
  455.4 68.4 %all-gather.11.cloned.1.call-start = ((), (), s32[]{:S(2)}) async-start(), calls=%async_computation.3 | async-start | bytes 1114112 | tf_op jit(solution)/shard_map/all_gather | solution.py:65
  483.1 297.4 %all-reduce.4.cloned.1.call-start = ((), (), s32[]{:S(2)}) async-start(), calls=%async_computation.4 | async-start | bytes 8388608 | tf_op jit(solution)/shard_map/psum | solution.py:15
Sparse Core Ops, SparseCore 0:
  9.0 28.2 all-gather.4
  39.4 153.2 all-gather.6
  455.5 25.7 all-gather.8
  483.4 40.3 all-gather.10
  676.3 104.1 all-reduce.3
where the time goes:
time: 823 us; the launch traced here: 820 us
  waiting for transfers between devices  355 us (43%)
  matrix products  280 us (34%)
  other arithmetic  134 us (16%)
  local copies, waits for them, and re-layouts  35.3 us (4%)
  between operations  16.1 us (2%)
    dot_general x1, matrix products, ntk_tile(): lax.dot_general(left_rows, right_rows, (((1,), (1,)), ((), ())), preferre...  252 us
    all_gather x1, waiting for transfers between devices, per_device(): every_row = lax.all_gather(row_feats, 'row', axis=0, tiled=True)  153 us
    psum x1, waiting for transfers between devices, broadcast(): return lax.psum(block, axis)  104 us
    another operation x14, other arithmetic, per_device(): corner_factor = jnp.linalg.cholesky(corner)  78.5 us
    all_gather x1, waiting for transfers between devices, per_device(): corner = lax.all_gather(panel_cols[:row_block], 'row', axis=0, tiled=True)  40.6 us
    another operation x3, other arithmetic, per_device(): lax.linalg.triangular_solve(corner_factor, panel_cols, left_side=False, l...  40 us
    all_gather x1, waiting for transfers between devices, per_device(): row_feats = lax.all_gather(samples, 'col', axis=0, tiled=True)  30 us
    all_gather x1, waiting for transfers between devices, per_device(): lax.all_gather(kernel[:, :col_block], 'col', axis=1, tiled=True)  25.9 us
  transfers between devices with their start and end apart: 5, of which 5 were waited for; matrix products, arithmetic and copies ran while one was open for 0% of the time, Pallas kernels for 0%

commit v1 on v0

v1 whole, which is shorter than its diff:
```python
import functools
import math

import jax
import jax.numpy as jnp
from jax import lax
from jax.experimental import pallas as pl
from jax.experimental.pallas import tpu as pltpu
from jax.sharding import PartitionSpec as P

FEAT = 768
PANEL = 512
LAYERS = 8
TILE_R = 128
TILE_C = 256
HIGH = lax.Precision.HIGHEST

ARC = (
    (4.501581511e-01, 3.751401299e-02, 8.424092758e-03, 2.633635570e-03, 4.183752006e-04, 1.140004682e-03, -6.902463010e-04, 4.019670222e-04),
    (4.501581511e-01, 3.751401299e-02, 8.424092758e-03, 2.633635570e-03, 4.183752006e-04, 1.140004682e-03, -6.902463010e-04, 4.019670222e-04),
    (4.501581596e-01, 3.751297114e-02, 8.445134407e-03, 2.473200384e-03, 1.005950977e-03, 2.413872371e-05, 3.721950193e-04),
    (4.501581559e-01, 3.751348376e-02, 8.433736400e-03, 2.565977952e-03, 6.640548863e-04, 6.060103696e-04),
    (4.501581678e-01, 3.751198578e-02, 8.463767294e-03, 2.355179154e-03, 1.268131146e-03),
    (4.501581611e-01, 3.751271895e-02, 8.451689076e-03, 2.417491958e-03, 1.169168271e-03),
    (4.501581592e-01, 3.751297767e-02, 8.446445380e-03, 2.450729231e-03, 1.104390918e-03),
    (4.501581377e-01, 3.751604518e-02, 8.377770913e-03, 2.943260388e-03),
)


def polynomial(coefs, d):
    value = jnp.full_like(d, coefs[-1])
    for coef in coefs[-2::-1]:
        value = value * d + coef
    return value


def tangent_of(cosine, tangent):
    for layer in range(LAYERS):
        size = jnp.abs(cosine) if layer == 0 else cosine
        d = jnp.maximum(1.0 - size, 1e-30)
        w = d * lax.rsqrt(d)
        e = size * (1.0 / math.pi**2) + 1.0 / math.pi**2
        sine = w * (e * lax.rsqrt(e))
        arc = w * polynomial(ARC[layer], d)
        rest = 1.0 - arc
        if layer == 0:
            rest = jnp.where(cosine < 0.0, arc, rest)
        cosine = sine + rest * cosine
        tangent = cosine + tangent * rest
    return tangent


def squares(x):
    xf = x.astype(jnp.float32)
    sq = xf * xf
    hi = sq.astype(jnp.bfloat16)
    lo = (sq - hi.astype(jnp.float32)).astype(jnp.bfloat16)
    return hi, lo


def dot_nt(a, b, precision=None):
    return lax.dot_general(
        a, b, (((1,), (1,)), ((), ())), precision=precision, preferred_element_type=jnp.float32
    )


def norms_down(x):
    hi, lo = squares(x)
    ones = jnp.ones((128, x.shape[1]), jnp.bfloat16)
    return dot_nt(hi, ones) + dot_nt(lo, ones)


def norms_across(x):
    hi, lo = squares(x)
    ones = jnp.ones((16, x.shape[1]), jnp.bfloat16)
    return (dot_nt(ones, hi) + dot_nt(ones, lo))[:8]


SCALE = 1.0 / math.sqrt(FEAT * (LAYERS + 1.0))


def in_order(x):
    return jnp.concatenate(
        [x[m * 128 + a * 32 : m * 128 + a * 32 + 32] for a in range(4) for m in range(2)], axis=0
    )


def factor_kernel(where_ref, lead_ref, own_ref, out_ref, mat, work, inv_dn, scl_dn, inv_ac, scl_ac):
    row_index = where_ref[0]
    col_index = where_ref[1]

    def norms(x_ref, start, count, across):
        x = x_ref[...]
        n = norms_down(x)
        r = lax.rsqrt(n)
        inv_dn[start : start + count, :] = r
        scl_dn[start : start + count, :] = n * r * SCALE
        if across:
            n = norms_across(x)
            r = lax.rsqrt(n)
            inv_ac[...] = r
            scl_ac[...] = n * r * SCALE

    norms(lead_ref, 0, PANEL, True)
    norms(own_ref, PANEL, 128, False)
    chunk = 64
    for jb in range(4):
        lanes = slice(jb * 128, jb * 128 + 128)
        cols = lead_ref[lanes, :]
        mat[jb * 128 : PANEL, lanes] = dot_nt(lead_ref[jb * 128 :, :], cols)
        mat[PANEL:, lanes] = dot_nt(own_ref[...], cols)
        inv_c = inv_ac[0:1, lanes]
        scl_c = scl_ac[0:1, lanes]

        def body(step, carry):
            start = pl.multiple_of(step * chunk, chunk)
            rows = pl.ds(start, chunk)
            raw = mat[rows, lanes] * inv_dn[rows, :] * inv_c
            local = start + lax.broadcasted_iota(jnp.int32, (chunk, 128), 0)
            own = local - PANEL
            own_block = own // 32
            own_id = (col_index * 4 + own_block) * PANEL + row_index * 32 + own - own_block * 32
            row_id = jnp.where(local < PANEL, local, own_id)
            col_id = jb * 128 + lax.broadcasted_iota(jnp.int32, (chunk, 128), 1)
            on_diag = row_id == col_id
            tangent = tangent_of(jnp.where(on_diag, 1.0, raw), raw)
            mat[rows, lanes] = tangent * scl_dn[rows, :] * scl_c + jnp.where(on_diag, 1.0, 0.0)
            return carry

        lax.fori_loop(jb * (128 // chunk), 640 // chunk, body, 0)

    lane = lax.broadcasted_iota(jnp.int32, (128, 128), 1)
    sub = lax.broadcasted_iota(jnp.int32, (128, 128), 0)
    eye = jnp.where(lane == sub, 1.0, 0.0)
    sub8 = lax.broadcasted_iota(jnp.int32, (8, 256), 0)
    for kb in range(4):
        lanes = slice(kb * 128, kb * 128 + 128)
        work[:, :128] = mat[lanes, lanes]
        work[:, 128:] = eye
        for jb in range(16):
            j = jb * 8
            rows = [jnp.broadcast_to(work[j + p : j + p + 1, :], (8, 256)) for p in range(8)]
            e = [[None] * 8 for _ in range(8)]
            for p in range(8):
                for q in range(p, 8):
                    e[p][q] = jnp.broadcast_to(rows[p][:, j + q : j + q + 1], (8, 128))
            block = None
            done = []
            for p in range(8):
                rinv = lax.rsqrt(e[p][p])
                for q in range(p + 1, 8):
                    e[p][q] = e[p][q] * rinv
                for q in range(p + 1, 8):
                    for s in range(q, 8):
                        e[q][s] = e[q][s] - e[p][q] * e[p][s]
                row = rows[p]
                for m in range(p):
                    row = row - jnp.concatenate([e[m][p]] * 2, axis=1) * done[m]
                row = row * jnp.concatenate([rinv] * 2, axis=1)
                done.append(row)
                block = row if p == 0 else jnp.where(sub8 == p, row, block)
            work[j : j + 8, :] = block
            if jb < 15:
                outer = lax.dot_general(
                    block[:, :128], block, (((0,), (0,)), ((), ())), precision=HIGH,
                    preferred_element_type=jnp.float32,
                )
                work[j + 8 :, :] = work[j + 8 :, :] - outer[j + 8 :, :]
        linv = work[:, 128:]
        below = (kb + 1) * 128
        solved = dot_nt(mat[below:, lanes], linv, HIGH)
        mine = solved[PANEL - below :, :]
        hi = mine.astype(jnp.bfloat16)
        out_ref[:, lanes] = hi
        out_ref[:, PANEL + kb * 128 : PANEL + kb * 128 + 128] = (
            mine - hi.astype(jnp.float32)
        ).astype(jnp.bfloat16)
        if kb < 3:
            mat[below:, below:] = mat[below:, below:] - dot_nt(solved, solved[: PANEL - below], HIGH)


def factor(where, lead, own):
    return pl.pallas_call(
        factor_kernel,
        out_shape=jax.ShapeDtypeStruct((128, 2 * PANEL), jnp.bfloat16),
        in_specs=[
            pl.BlockSpec(memory_space=pltpu.SMEM),
            pl.BlockSpec(memory_space=pltpu.VMEM),
            pl.BlockSpec(memory_space=pltpu.VMEM),
        ],
        out_specs=pl.BlockSpec(memory_space=pltpu.VMEM),
        scratch_shapes=[
            pltpu.VMEM((PANEL + 128, PANEL), jnp.float32),
            pltpu.VMEM((128, 256), jnp.float32),
            pltpu.VMEM((PANEL + 128, 128), jnp.float32),
            pltpu.VMEM((PANEL + 128, 128), jnp.float32),
            pltpu.VMEM((8, PANEL), jnp.float32),
            pltpu.VMEM((8, PANEL), jnp.float32),
        ],
        name="factor",
        cost_estimate=pl.CostEstimate(flops=int(1e9), bytes_accessed=int(2e6), transcendentals=0),
    )(where, lead, own)


def tiles_kernel(where_ref, rows_ref, cols_ref, out_ref, cols, gram, inv_ac, scl_ac, inv_dn, scl_dn):
    step = pl.program_id(0)
    row_index = where_ref[0]
    col_index = where_ref[1]
    count = cols_ref.shape[0] // TILE_C

    @pl.when(step == 0)
    def _():
        def body(t, carry):
            rows = pl.ds(pl.multiple_of(t * TILE_C, TILE_C), TILE_C)
            x = in_order(cols_ref[rows, :])
            cols[rows, :] = x
            n = norms_across(x)
            r = lax.rsqrt(n)
            inv_ac[t] = r
            scl_ac[t] = n * r * SCALE
            return carry

        lax.fori_loop(0, count, body, 0)

    x = rows_ref[...]
    n = norms_down(x)
    r = lax.rsqrt(n)
    inv_dn[...] = r
    scl_dn[...] = n * r * SCALE

    def tile(t, carry):
        start = pl.multiple_of(t * TILE_C, TILE_C)
        gram[...] = dot_nt(x, cols[pl.ds(start, TILE_C), :])
        inv_c = inv_ac[t][0:1]
        scl_c = scl_ac[t][0:1]
        chunk = 32

        def body(k, carry, diag):
            first = pl.multiple_of(k * chunk, chunk)
            rows = pl.ds(first, chunk)
            inv_r = jnp.concatenate([inv_dn[rows, :]] * 2, axis=1)
            scl_r = jnp.concatenate([scl_dn[rows, :]] * 2, axis=1)
            raw = gram[rows, :] * inv_r * inv_c
            if diag:
                u = lax.broadcasted_iota(jnp.int32, (chunk, TILE_C), 0)
                v = lax.broadcasted_iota(jnp.int32, (chunk, TILE_C), 1)
                row_id = (step * 4 + k) * PANEL + row_index * 32 + u
                col_id = (t * 4 + v // 64) * PANEL + col_index * 64 + v % 64
                on_diag = row_id == col_id
                tangent = tangent_of(jnp.where(on_diag, 1.0, raw), raw)
                value = tangent * scl_r * scl_c + jnp.where(on_diag, 1.0, 0.0)
            else:
                value = tangent_of(raw, raw) * scl_r * scl_c
            out_ref[rows, pl.ds(start, TILE_C)] = value
            return carry

        @pl.when(t == step)
        def _():
            lax.fori_loop(0, TILE_R // chunk, functools.partial(body, diag=True), 0)

        @pl.when(t != step)
        def _():
            lax.fori_loop(0, TILE_R // chunk, functools.partial(body, diag=False), 0)

        return carry

    lax.fori_loop(0, step + 1, tile, 0)


def tiles(where, rows, cols):
    n_rows, n_cols = rows.shape[0], cols.shape[0]
    return pl.pallas_call(
        tiles_kernel,
        out_shape=jax.ShapeDtypeStruct((n_rows, n_cols), jnp.float32),
        grid=(n_rows // TILE_R,),
        in_specs=[
            pl.BlockSpec(memory_space=pltpu.SMEM),
            pl.BlockSpec((TILE_R, FEAT), lambda i: (i, 0)),
            pl.BlockSpec((n_cols, FEAT), lambda i: (0, 0)),
        ],
        out_specs=pl.BlockSpec((TILE_R, n_cols), lambda i: (i, 0)),
        scratch_shapes=[
            pltpu.VMEM((n_cols, FEAT), jnp.bfloat16),
            pltpu.VMEM((TILE_R, TILE_C), jnp.float32),
            pltpu.VMEM((n_cols // TILE_C, 8, TILE_C), jnp.float32),
            pltpu.VMEM((n_cols // TILE_C, 8, TILE_C), jnp.float32),
            pltpu.VMEM((TILE_R, 128), jnp.float32),
            pltpu.VMEM((TILE_R, 128), jnp.float32),
        ],
        name="tiles",
        cost_estimate=pl.CostEstimate(flops=int(30e9), bytes_accessed=int(12e6), transcendentals=0),
    )(where, rows, cols)


def update_kernel(where_ref, kernel_ref, rows_ref, cols_ref, out_ref):
    step = pl.program_id(0)
    row_index = where_ref[0]
    col_index = where_ref[1]
    count = cols_ref.shape[0] // TILE_C
    for half in range(2):
        row_tile = step * 2 + half
        mine = slice(half * TILE_R, half * TILE_R + TILE_R)
        hi_r = rows_ref[mine, :PANEL]
        lo_r = rows_ref[mine, PANEL:]
        for t in range(count):
            lanes = slice(t * TILE_C, t * TILE_C + TILE_C)

            @pl.when(row_tile < t)
            def _():
                out_ref[mine, lanes] = jnp.zeros((TILE_R, TILE_C), jnp.float32)

            @pl.when(row_tile >= t)
            def _():
                both = in_order(cols_ref[lanes, :])
                hi_c = both[:, :PANEL]
                lo_c = both[:, PANEL:]
                drop = dot_nt(hi_r, hi_c) + dot_nt(hi_r, lo_c) + dot_nt(lo_r, hi_c)
                value = kernel_ref[mine, lanes] - drop
                s = lax.broadcasted_iota(jnp.int32, (TILE_R, TILE_C), 0)
                v = lax.broadcasted_iota(jnp.int32, (TILE_R, TILE_C), 1)
                if t == 0:
                    first = pl.multiple_of(col_index // 2 * 128, 128)
                    left = rows_ref[mine, pl.ds(first, 128)].astype(jnp.float32)
                    left = left + rows_ref[mine, pl.ds(first + PANEL, 128)].astype(jnp.float32)
                    left = jnp.where(col_index % 2 == 1, pltpu.roll(left, 64, 1), left)
                    left = jnp.concatenate([left, left], axis=1)
                    value = jnp.where(v < 64, left, value)
                row_id = (row_tile * 4 + s // 32) * PANEL + row_index * 32 + s % 32
                col_id = (t * 4 + v // 64) * PANEL + col_index * 64 + v % 64
                out_ref[mine, lanes] = jnp.where(row_id >= col_id, value, 0.0)


def update(where, kernel, rows, cols):
    n_rows, n_cols = kernel.shape
    return pl.pallas_call(
        update_kernel,
        out_shape=jax.ShapeDtypeStruct((n_rows, n_cols), jnp.float32),
        grid=(n_rows // (2 * TILE_R),),
        in_specs=[
            pl.BlockSpec(memory_space=pltpu.SMEM),
            pl.BlockSpec((2 * TILE_R, n_cols), lambda i: (i, 0)),
            pl.BlockSpec((2 * TILE_R, 2 * PANEL), lambda i: (i, 0)),
            pl.BlockSpec((n_cols, 2 * PANEL), lambda i: (0, 0)),
        ],
        out_specs=pl.BlockSpec((2 * TILE_R, n_cols), lambda i: (i, 0)),
        name="update",
        cost_estimate=pl.CostEstimate(flops=int(6e9), bytes_accessed=int(20e6), transcendentals=0),
    )(where, kernel, rows, cols)


def per_device(samples):
    row_count = lax.axis_size("row")
    col_count = lax.axis_size("col")
    where = jnp.stack([lax.axis_index("row"), lax.axis_index("col")]).astype(jnp.int32)
    share = row_count // col_count
    route = [
        (r * col_count + k, (k * share + r % share) * col_count + r // share)
        for r in range(row_count)
        for k in range(col_count)
    ]

    def to_columns(x):
        moved = lax.ppermute(x, ("row", "col"), route)
        return lax.all_gather(moved, "row", axis=0, tiled=True)

    head = lax.all_gather(samples[: PANEL // row_count], "col", axis=0)[0]
    lead = lax.all_gather(head, "row", axis=0, tiled=True)
    row_feats = lax.all_gather(samples, "col", axis=0, tiled=True)
    col_feats = to_columns(samples)
    mine = factor(where, lead, samples)
    panel_row = lax.all_gather(mine, "col", axis=0, tiled=True)
    panel_col = to_columns(mine)
    kernel = tiles(where, row_feats, col_feats)
    return update(where, kernel, panel_row, panel_col)


def solution(mesh):
    return jax.shard_map(
        per_device,
        mesh=mesh,
        in_specs=(P(("row", "col"), None),),
        out_specs=P("row", "col"),
        check_vma=False,
    )
```

time: 823 us -> 223 us (0.27)
  waiting for transfers between devices: 355 us -> 21 us
  matrix products: 280 us -> 0 us
  other arithmetic: 134 us -> 0.59 us
  Pallas kernels: 0 us -> 127 us
  blocking collectives: 0 us -> 44.7 us
  local copies, waits for them, and re-layouts: 35.3 us -> 2.21 us
  starting transfers between devices: 0.16 us -> 14.2 us
    dot_general x2 -> x0, matrix products: 269 us -> none  [the longest x1 252 us: ntk_tile(): lax.dot_general(left_rows, right_rows, (((1,), (1,)), ((), ())), preferre...]
    all_gather x3, waiting for transfers between devices: 220 us -> 12.4 us  [the longest x2 12.4 us: to_columns(): return lax.all_gather(moved, 'row', axis=0, tiled=True)]
    pallas_call x0 -> x3, Pallas kernels: none -> 127 us  [the longest x1 57.6 us: tiles(): pl.pallas_call(tiles_kernel, out_shape=jax.ShapeDtypeStruct((n_rows, n_co...]
    another operation x18 -> x1, other arithmetic: 121 us -> 0.59 us  [per_device(): jnp.stack([lax.axis_index('row'), lax.axis_index('col')]).astype(jnp.int32)]
    psum x1 -> x0, waiting for transfers between devices: 104 us -> none  [broadcast(): return lax.psum(block, axis)]
    all_gather x0 -> x2, blocking collectives: none -> 44.7 us  [the longest x1 23.5 us: per_device(): head = lax.all_gather(samples[:PANEL // row_count], 'col', axis=0)[0]]
    all_gather x1, waiting for transfers between devices: 30 us -> 0.02 us  [per_device(): row_feats = lax.all_gather(samples, 'col', axis=0, tiled=True)]
    select_n x3 -> x0, local copies, waits for them, and re-layouts: 15 us -> none  [the longest x1 9.12 us: per_device(): jnp.where(row_ids[:, None] >= col_ids[None, :], result, jnp.float32(0.0))]
  transfers between devices with their start and end apart: 5 -> 6, of which waited for: 5 -> 3; matrix products, arithmetic and copies ran while one was open for 0% -> 1% of each run, Pallas kernels for 0% -> 48%
where the time goes in v1:
time: 223 us; the launch traced here: 222 us
  Pallas kernels  127 us (57%)
  blocking collectives  44.7 us (20%)
  waiting for transfers between devices  21 us (9%)
  starting transfers between devices  14.2 us (6%)
  between operations  13.2 us (6%)
    pallas_call x1, Pallas kernels, tiles(): pl.pallas_call(tiles_kernel, out_shape=jax.ShapeDtypeStruct((n_rows, n_co...  57.6 us
    pallas_call x1, Pallas kernels, factor(): pl.pallas_call(factor_kernel, out_shape=jax.ShapeDtypeStruct((128, 2 * PA...  49.8 us
    all_gather x1, blocking collectives, per_device(): head = lax.all_gather(samples[:PANEL // row_count], 'col', axis=0)[0]  23.5 us
    all_gather x1, blocking collectives, per_device(): lead = lax.all_gather(head, 'row', axis=0, tiled=True)  21.2 us
    pallas_call x1, Pallas kernels, update(): pl.pallas_call(update_kernel, out_shape=jax.ShapeDtypeStruct((n_rows, n_c...  19.2 us
    ppermute x2, starting transfers between devices, to_columns(): moved = lax.ppermute(x, ('row', 'col'), route)  14.1 us
    all_gather x2, waiting for transfers between devices, to_columns(): return lax.all_gather(moved, 'row', axis=0, tiled=True)  12.4 us
    ppermute x2, waiting for transfers between devices, to_columns(): moved = lax.ppermute(x, ('row', 'col'), route)  7.8 us
  transfers between devices with their start and end apart: 6, of which 3 were waited for; matrix products, arithmetic and copies ran while one was open for 1% of the time, Pallas kernels for 48%

profile of v1, /device:TPU:1, one launch (start us, length us, event | category | flops | bytes accessed | tf_op | source)
XLA Modules:
  0.0 222.5 jit_solution(10520743599771004518)
XLA Ops:
  6.5 0.0 all-gather.8.cloned.1.call-start
  6.5 0.7 all-gather.8.cloned.1.call-update
  7.3 0.0 all-gather.10.cloned.1.call-start
  7.3 6.0 %collective-permute-start = (bf16[128,768]{1,0:T(8,128)(2,1)}, bf16[128,768]{1,0:T(8,128)(2,1)S(1)}, u32[]{:S(2)}, u32[]{:S(2)}) collective-permute-start(bf16[128,768]{1,0:T(8,128)(2,1)} %own_ref.1), channel_id=1, source_target_pairs={{0,0},{1,16},{2,32},{3,48},{4,64},{5,80},{6,96},{7,112},{8,8},{9,2... | collective-permute-start | bytes 589832 | tf_op jit(solution)/shard_map/ppermute | solution.py:363
  13.3 3.5 %collective-permute-done = bf16[128,768]{1,0:T(8,128)(2,1)S(1)} collective-permute-done((bf16[128,768]{1,0:T(8,128)(2,1)}, bf16[128,768]{1,0:T(8,128)(2,1)S(1)}, u32[]{:S(2)}, u32[]{:S(2)}) %collective-permute-start) | collective-permute-done | bytes 196640 | tf_op jit(solution)/shard_map/ppermute | solution.py:363
  16.9 0.7 copy-done.1
  17.6 0.0 all-gather.10.cloned.1.call-update
  17.6 0.0 all-gather.12.cloned.1.call-start
  17.7 0.8 slice.6
  18.5 23.5 %all-gather = bf16[256,768]{1,0:T(8,128)(2,1)S(1)} all-gather(bf16[32,768]{1,0:T(8,128)(2,1)S(1)} %slice.6), channel_id=2, replica_groups=mesh['row'=16,'col'=8] {'col'}, dimensions={0}, use_global_device_ids=true | all-gather | bytes 442368 | tf_op jit(solution)/shard_map/all_gather | solution.py:366
  41.9 0.6 pad_add_fusion.where_ref
  42.5 21.2 %all-gather.2.lead_ref = bf16[512,768]{1,0:T(8,128)(2,1)} all-gather(bf16[32,768]{1,0:T(8,128)(2,1)S(1)} %slice.9), channel_id=4, replica_groups=mesh['row'=16,'col'=8] {'row'}, dimensions={0}, use_global_device_ids=true | all-gather | bytes 835584 | tf_op jit(solution)/shard_map/all_gather | solution.py:367
  63.7 49.8 %factor.1 = bf16[128,1024]{1,0:T(8,128)(2,1)} custom-call(s32[2]{0:T(128)} %pad_add_fusion.where_ref, bf16[512,768]{1,0:T(8,128)(2,1)} %all-gather.2.lead_ref, bf16[128,768]{1,0:T(8,128)(2,1)} %own_ref.1), custom_call_target="tpu_custom_call" | custom-call | flops 1000000000 | bytes 2000000 | tf_op jit(solution)/shard_map/factor/pallas_call | solution.py:183
  113.5 0.0 all-gather.12.cloned.1.call-update
  113.6 0.0 all-gather.14.cloned.1.call-start
  113.6 8.0 %collective-permute-start.1 = (bf16[128,1024]{1,0:T(8,128)(2,1)}, bf16[128,1024]{1,0:T(8,128)(2,1)S(1)}, u32[]{:S(2)}, u32[]{:S(2)}) collective-permute-start(bf16[128,1024]{1,0:T(8,128)(2,1)} %factor.1), channel_id=1, source_target_pairs={{0,0},{1,16},{2,32},{3,48},{4,64},{5,80},{6,96},{7,112},{8,8},{9,2... | collective-permute-start | bytes 786440 | tf_op jit(solution)/shard_map/ppermute | solution.py:363
  121.7 4.3 %collective-permute-done.1 = bf16[128,1024]{1,0:T(8,128)(2,1)S(1)} collective-permute-done((bf16[128,1024]{1,0:T(8,128)(2,1)}, bf16[128,1024]{1,0:T(8,128)(2,1)S(1)}, u32[]{:S(2)}, u32[]{:S(2)}) %collective-permute-start.1) | collective-permute-done | bytes 262176 | tf_op jit(solution)/shard_map/ppermute | solution.py:363
  125.9 0.7 copy-done
  126.6 0.0 all-gather.14.cloned.1.call-update
  126.6 0.0 all-gather.8.cloned.1.call-done.rows_ref
  126.7 0.0 all-gather.10.cloned.1.call-done.cols_ref
  126.7 57.6 %tiles.1.kernel_ref = f32[1024,2048]{1,0:T(8,128)} custom-call(s32[2]{0:T(128)} %pad_add_fusion.where_ref, bf16[1024,768]{1,0:T(8,128)(2,1)} %all-gather.8.cloned.1.call-done.rows_ref, bf16[2048,768]{1,0:T(8,128)(2,1)} %all-gather.10.cloned.1.call-done.cols_ref), custom_call_target="tpu_custom_call" | custom-call | flops 30000001024 | bytes 12000000 | tf_op jit(solution)/shard_map/tiles/pallas_call | solution.py:272
  184.3 12.4 %all-gather.14.cloned.1.call-done.cols_ref = bf16[2048,1024]{1,0:T(8,128)(2,1)} async-done(((bf16[128,1024]{1,0:T(8,128)(2,1)}), bf16[2048,1024]{1,0:T(8,128)(2,1)}) %all-gather.14.cloned.1.call-update) | async-done | bytes 4194320 | tf_op jit(solution)/shard_map/all_gather | solution.py:364
  196.7 19.2 %update.1 = f32[1024,2048]{1,0:T(8,128)} custom-call(s32[2]{0:T(128)} %pad_add_fusion.where_ref, f32[1024,2048]{1,0:T(8,128)} %tiles.1.kernel_ref, bf16[1024,1024]{1,0:T(8,128)(2,1)} %all-gather.12.cloned.1.call-done.rows_ref, bf16[2048,1024]{1,0:T(8,128)(2,1)} %all-gather.14.cloned.1.call-done.cols_ref), custom_call_target="tpu_custom_call" | custom-call | flops 6000000000 | bytes 20000000 | tf_op jit(solution)/shard_map/update/pallas_call | solution.py:335
  (4 shorter events, 0.0 us)
Async XLA Ops:
  6.5 120.1 %all-gather.8.cloned.1.call-start = ((), (), s32[]{:S(2)}) async-start(), calls=%async_computation | async-start | bytes 1769472 | tf_op jit(solution)/shard_map/all_gather | solution.py:368
  7.3 119.4 %all-gather.10.cloned.1.call-start = ((), (), s32[]{:S(2)}) async-start(), calls=%async_computation.1 | async-start | bytes 3342336 | tf_op jit(solution)/shard_map/all_gather | solution.py:364
  7.3 9.6 %collective-permute-start = (bf16[128,768]{1,0:T(8,128)(2,1)}, bf16[128,768]{1,0:T(8,128)(2,1)S(1)}, u32[]{:S(2)}, u32[]{:S(2)}) collective-permute-start(bf16[128,768]{1,0:T(8,128)(2,1)} %own_ref.1), channel_id=1, source_target_pairs={{0,0},{1,16},{2,32},{3,48},{4,64},{5,80},{6,96},{7,112},{8,8},{9,2... | collective-permute-start | bytes 589832 | tf_op jit(solution)/shard_map/ppermute | solution.py:363
  16.9 0.7 copy-start.1
  17.6 166.7 %all-gather.12.cloned.1.call-start = ((), (), s32[]{:S(2)}) async-start(), calls=%async_computation.2 | async-start | bytes 2359296 | tf_op jit(solution)/shard_map/all_gather | solution.py:371
  113.6 83.2 %all-gather.14.cloned.1.call-start = ((), (), s32[]{:S(2)}) async-start(), calls=%async_computation.3 | async-start | bytes 4456448 | tf_op jit(solution)/shard_map/all_gather | solution.py:364
  113.6 12.3 %collective-permute-start.1 = (bf16[128,1024]{1,0:T(8,128)(2,1)}, bf16[128,1024]{1,0:T(8,128)(2,1)S(1)}, u32[]{:S(2)}, u32[]{:S(2)}) collective-permute-start(bf16[128,1024]{1,0:T(8,128)(2,1)} %factor.1), channel_id=1, source_target_pairs={{0,0},{1,16},{2,32},{3,48},{4,64},{5,80},{6,96},{7,112},{8,8},{9,2... | collective-permute-start | bytes 786440 | tf_op jit(solution)/shard_map/ppermute | solution.py:363
  125.9 0.7 copy-start
Sparse Core Ops, SparseCore 0:
  9.0 28.4 all-gather.7
  39.7 47.8 all-gather.9
  113.7 32.0 all-gather.11
  147.7 48.9 all-gather.13

commit v2 on v1

v2 whole, which is shorter than its diff:
```python
import functools
import math

import jax
import jax.numpy as jnp
import numpy as np
from jax import lax
from jax.experimental import pallas as pl
from jax.experimental.pallas import tpu as pltpu
from jax.sharding import PartitionSpec as P

FEAT = 768
PANEL = 512
LAYERS = 8
TILE_R = 128
TILE_C = 256
HIGH = lax.Precision.HIGHEST

ARC = (
    (1.570796265e+00, -9.999884905e-01, 7.850416849e-01, -6.623695706e-01, 5.625094387e-01, -4.372503233e-01, 2.693842319e-01, -1.086155413e-01, 2.049311747e-02),
    (1.570796265e+00, -9.999884905e-01, 7.850416849e-01, -6.623695706e-01, 5.625094387e-01, -4.372503233e-01, 2.693842319e-01, -1.086155413e-01, 2.049311747e-02),
    (1.570326531e+00, -9.935370566e-01, 7.471319178e-01, -5.376914312e-01, 3.111383121e-01, -1.187027540e-01, 2.133516172e-02),
    (1.567898155e+00, -9.719742948e-01, 6.682907781e-01, -3.857788817e-01, 1.484597498e-01, -2.689621130e-02),
    (1.566642297e+00, -9.635808948e-01, 6.460403822e-01, -3.565340200e-01, 1.294006162e-01, -2.196850873e-02),
    (1.558633208e+00, -9.141686374e-01, 5.246089379e-01, -2.079489415e-01, 3.887608390e-02),
    (1.557122831e+00, -9.070176865e-01, 5.119586953e-01, -1.980387362e-01, 3.597512846e-02),
    (1.555954084e+00, -9.016562063e-01, 5.027575168e-01, -1.910373211e-01, 3.398202014e-02),
)


def scales():
    out = [np.float32(1.0)]
    for _ in range(LAYERS):
        out.append(np.float32(np.float32(math.pi) * out[-1]))
    return out


KAPPA = scales()


def polynomial(coefs, c):
    value = c * coefs[-1] + coefs[-2]
    for coef in coefs[-3::-1]:
        value = value * c + coef
    return value


def tangent_of(cosine, tangent):
    for layer in range(LAYERS):
        kappa = KAPPA[layer]
        coefs = [float(a / np.float64(kappa) ** (k + 1)) for k, a in enumerate(ARC[layer])]
        size = jnp.abs(cosine) if layer == 0 else cosine
        square = jnp.maximum(float(np.float32(kappa * kappa)) - size * size, 1e-30)
        sine = square * lax.rsqrt(square)
        angle = sine * polynomial(coefs, size)
        rest = math.pi - angle
        if layer == 0:
            rest = jnp.where(cosine < 0.0, angle, rest)
        cosine = sine + rest * cosine
        tangent = cosine + rest * tangent
    return tangent


def squares(x):
    xf = x.astype(jnp.float32)
    sq = xf * xf
    hi = sq.astype(jnp.bfloat16)
    lo = (sq - hi.astype(jnp.float32)).astype(jnp.bfloat16)
    return hi, lo


def dot_nt(a, b, precision=None):
    return lax.dot_general(
        a, b, (((1,), (1,)), ((), ())), precision=precision, preferred_element_type=jnp.float32
    )


def norms_down(x):
    hi, lo = squares(x)
    ones = jnp.ones((128, x.shape[1]), jnp.bfloat16)
    return dot_nt(hi, ones) + dot_nt(lo, ones)


def norms_across(x):
    hi, lo = squares(x)
    ones = jnp.ones((16, x.shape[1]), jnp.bfloat16)
    return (dot_nt(ones, hi) + dot_nt(ones, lo))[:8]


SCALE = 1.0 / math.sqrt(FEAT * (LAYERS + 1.0) * float(KAPPA[LAYERS]))


def in_order(x):
    return jnp.concatenate(
        [x[m * 128 + a * 32 : m * 128 + a * 32 + 32] for a in range(4) for m in range(2)], axis=0
    )


def split(x):
    hi = x.astype(jnp.bfloat16)
    return hi, (x - hi.astype(jnp.float32)).astype(jnp.bfloat16)


def slot_of(step, where):
    other = (step + where[1]) % 2
    mine = where[1] + other * (1 - 2 * (where[1] % 2))
    return ((mine - step + 8) % 8) // 2, other


def leading_kernel(
    where_ref, g0, g1, g2, g3, own_ref, corner_ref, out_ref, lead, inv_dn, scl_dn, inv_ac, scl_ac
):
    row_index = where_ref[0]
    col_index = where_ref[1]
    for dx, piece in enumerate((g0, g1, g2, g3)):
        for dy in range(4):
            r = (row_index // 4 + 4 - dy) % 4 * 4 + (row_index % 4 + 4 - dx) % 4
            lead[pl.ds(pl.multiple_of(r * 32, 32), 32), :] = piece[dy]

    def norms(x, start, count):
        n = norms_down(x)
        r = lax.rsqrt(n)
        inv_dn[start : start + count, :] = r
        scl_dn[start : start + count, :] = n * r * SCALE

    x = lead[...]
    norms(x, 0, PANEL)
    n = norms_across(x)
    r = lax.rsqrt(n)
    inv_ac[...] = r
    scl_ac[...] = n * r * SCALE
    norms(own_ref[...], PANEL, 128)
    chunk = 64
    for jb in range(4):
        lanes = slice(jb * 128, jb * 128 + 128)
        cols = lead[lanes, :]
        corner_ref[jb * 128 :, lanes] = dot_nt(lead[jb * 128 :, :], cols)
        out_ref[:, lanes] = dot_nt(own_ref[...], cols)
        inv_c = inv_ac[0:1, lanes]
        scl_c = scl_ac[0:1, lanes]

        def body(step, carry, ref, base):
            start = pl.multiple_of(step * chunk, chunk)
            rows = pl.ds(start, chunk)
            down = pl.ds(start + base, chunk)
            raw = ref[rows, lanes] * inv_dn[down, :] * inv_c
            local = start + lax.broadcasted_iota(jnp.int32, (chunk, 128), 0)
            if base:
                block = local // 32
                local = (col_index * 4 + block) * PANEL + row_index * 32 + local - block * 32
            col_id = jb * 128 + lax.broadcasted_iota(jnp.int32, (chunk, 128), 1)
            on_diag = local == col_id
            tangent = tangent_of(jnp.where(on_diag, 1.0, raw), raw)
            ref[rows, lanes] = tangent * scl_dn[down, :] * scl_c + jnp.where(on_diag, 1.0, 0.0)
            return carry

        lax.fori_loop(0, 128 // chunk, functools.partial(body, ref=out_ref, base=PANEL), 0, unroll=2)
        lax.fori_loop(
            jb * (128 // chunk), PANEL // chunk, functools.partial(body, ref=corner_ref, base=0), 0
        )


def leading(where, pieces, own):
    vmem = pl.BlockSpec(memory_space=pltpu.VMEM)
    return pl.pallas_call(
        leading_kernel,
        out_shape=(
            jax.ShapeDtypeStruct((PANEL, PANEL), jnp.float32),
            jax.ShapeDtypeStruct((128, PANEL), jnp.float32),
        ),
        in_specs=[pl.BlockSpec(memory_space=pltpu.SMEM)] + [vmem] * 5,
        out_specs=(vmem, vmem),
        scratch_shapes=[
            pltpu.VMEM((PANEL, FEAT), jnp.bfloat16),
            pltpu.VMEM((PANEL + 128, 128), jnp.float32),
            pltpu.VMEM((PANEL + 128, 128), jnp.float32),
            pltpu.VMEM((8, PANEL), jnp.float32),
            pltpu.VMEM((8, PANEL), jnp.float32),
        ],
        name="leading",
        cost_estimate=pl.CostEstimate(flops=int(8e9), bytes_accessed=int(2e6), transcendentals=0),
    )(where, *pieces, own)


def factor_kernel(corner_ref, out_ref, mat, work):
    eye = jnp.where(
        lax.broadcasted_iota(jnp.int32, (128, 128), 1)
        == lax.broadcasted_iota(jnp.int32, (128, 128), 0),
        1.0,
        0.0,
    )
    sub8 = lax.broadcasted_iota(jnp.int32, (8, 256), 0)
    mat[:PANEL, :] = corner_ref[...]
    mat[PANEL:, :] = jnp.zeros((PANEL, PANEL), jnp.float32)

    def eliminate(kb):
        lanes = slice(kb * 128, kb * 128 + 128)
        linv = work[:, 128:]
        inverse = jnp.transpose(linv)
        top = PANEL + kb * 128
        if kb:
            upper = dot_nt(mat[PANEL:top, lanes], linv, HIGH)
            mat[PANEL:top, lanes] = upper
            upper = jnp.concatenate([upper, inverse], axis=0)
        else:
            upper = inverse
        mat[top : top + 128, lanes] = inverse
        if kb < 3:
            below = (kb + 1) * 128
            solved = dot_nt(mat[below:PANEL, lanes], linv, HIGH)
            mat[below:PANEL, below:] = mat[below:PANEL, below:] - dot_nt(solved, solved, HIGH)
            mat[PANEL : top + 128, below:] = mat[PANEL : top + 128, below:] - dot_nt(
                upper, solved, HIGH
            )

    def column(kb, carry):
        first = pl.multiple_of(kb * 128, 128)
        work[:, :128] = mat[pl.ds(first, 128), pl.ds(first, 128)]
        work[:, 128:] = eye
        for jb in range(16):
            j = jb * 8
            rows = [jnp.broadcast_to(work[j + p : j + p + 1, :], (8, 256)) for p in range(8)]
            e = [[None] * 8 for _ in range(8)]
            for p in range(8):
                for q in range(p, 8):
                    e[p][q] = jnp.broadcast_to(rows[p][:, j + q : j + q + 1], (8, 128))
            block = None
            done = []
            for p in range(8):
                rinv = lax.rsqrt(e[p][p])
                for q in range(p + 1, 8):
                    e[p][q] = e[p][q] * rinv
                for q in range(p + 1, 8):
                    for s in range(q, 8):
                        e[q][s] = e[q][s] - e[p][q] * e[p][s]
                row = rows[p]
                for m in range(p):
                    row = row - jnp.concatenate([e[m][p]] * 2, axis=1) * done[m]
                row = row * jnp.concatenate([rinv] * 2, axis=1)
                done.append(row)
                block = row if p == 0 else jnp.where(sub8 == p, row, block)
            work[j : j + 8, :] = block
            if jb < 15:
                outer = lax.dot_general(
                    block[:, :128], block, (((0,), (0,)), ((), ())), precision=HIGH,
                    preferred_element_type=jnp.float32,
                )
                work[j + 8 :, :] = work[j + 8 :, :] - outer[j + 8 :, :]
        for n in range(4):
            pl.when(kb == n)(functools.partial(eliminate, n))
        return carry

    lax.fori_loop(0, 4, column, 0)
    hi, lo = split(mat[PANEL:, :])
    out_ref[:, :PANEL] = hi
    out_ref[:, PANEL:] = lo


def factor(corner):
    return pl.pallas_call(
        factor_kernel,
        out_shape=jax.ShapeDtypeStruct((PANEL, 2 * PANEL), jnp.bfloat16),
        in_specs=[pl.BlockSpec(memory_space=pltpu.VMEM)],
        out_specs=pl.BlockSpec(memory_space=pltpu.VMEM),
        scratch_shapes=[
            pltpu.VMEM((2 * PANEL, PANEL), jnp.float32),
            pltpu.VMEM((128, 256), jnp.float32),
        ],
        name="factor",
        cost_estimate=pl.CostEstimate(flops=int(25e9), bytes_accessed=int(2e6), transcendentals=0),
    )(corner)


def tiles_kernel(
    where_ref, near_ref, far_ref, cols_ref, out_ref, cols, gram, inv_ac, scl_ac, inv_dn, scl_dn
):
    step = pl.program_id(0)
    row_index = where_ref[0]
    col_index = where_ref[1]
    count = cols_ref.shape[0] // TILE_C

    @pl.when(step == 0)
    def _():
        def body(t, carry):
            rows = pl.ds(pl.multiple_of(t * TILE_C, TILE_C), TILE_C)
            x = in_order(cols_ref[rows, :])
            cols[rows, :] = x
            n = norms_across(x)
            r = lax.rsqrt(n)
            inv_ac[t] = r
            scl_ac[t] = n * r * SCALE
            return carry

        lax.fori_loop(0, count, body, 0)

    _, other = slot_of(step, where_ref)
    x = jnp.where(other == 1, far_ref[0], near_ref[0])
    n = norms_down(x)
    r = lax.rsqrt(n)
    inv_dn[...] = r
    scl_dn[...] = n * r * SCALE
    chunk = 32

    def product(t, slot):
        start = pl.multiple_of(t * TILE_C, TILE_C)
        gram[slot] = dot_nt(x, cols[pl.ds(start, TILE_C), :])

    def piece(t, slot, k):
        rows = slice(k * chunk, k * chunk + chunk)
        inv_r = jnp.concatenate([inv_dn[rows, :]] * 2, axis=1)
        scl_r = jnp.concatenate([scl_dn[rows, :]] * 2, axis=1)
        raw = gram[slot, rows, :] * inv_r * inv_ac[t][0:1]
        value = tangent_of(raw, raw) * scl_r * scl_ac[t][0:1]
        out_ref[rows, pl.ds(pl.multiple_of(t * TILE_C, TILE_C), TILE_C)] = value

    product(0, 0)

    def tile(t, carry):
        slot = t % 2
        product(t + 1, 1 - slot)
        for k in range(TILE_R // chunk):
            piece(t, slot, k)
        return carry

    lax.fori_loop(0, step, tile, 0)

    slot = step % 2
    for half in range(2):
        width = 128 * (half + 1)
        rows = slice(half * 64, half * 64 + 64)
        for lane in range(half + 1):
            lanes = slice(lane * 128, lane * 128 + 128)
            raw = gram[slot, rows, lanes] * inv_dn[rows, :] * inv_ac[step][0:1, lanes]
            u = half * 64 + lax.broadcasted_iota(jnp.int32, (64, 128), 0)
            v = lane * 128 + lax.broadcasted_iota(jnp.int32, (64, 128), 1)
            row_id = u // 32 * PANEL + row_index * 32 + u % 32
            col_id = v // 64 * PANEL + col_index * 64 + v % 64
            on_diag = row_id == col_id
            tangent = tangent_of(jnp.where(on_diag, 1.0, raw), raw)
            value = tangent * scl_dn[rows, :] * scl_ac[step][0:1, lanes]
            value = value + jnp.where(on_diag, 1.0, 0.0)
            first = pl.multiple_of(step * TILE_C + lane * 128, 128)
            out_ref[rows, pl.ds(first, 128)] = value


def tiles(where, near, far, cols):
    n_rows, n_cols = 8 * TILE_R, cols.shape[0]
    piece = (1, TILE_R, FEAT)
    return pl.pallas_call(
        tiles_kernel,
        out_shape=jax.ShapeDtypeStruct((n_rows, n_cols), jnp.float32),
        grid_spec=pltpu.PrefetchScalarGridSpec(
            num_scalar_prefetch=1,
            grid=(n_rows // TILE_R,),
            in_specs=[
                pl.BlockSpec(piece, lambda i, where: (slot_of(i, where)[0], 0, 0)),
                pl.BlockSpec(piece, lambda i, where: (slot_of(i, where)[0], 0, 0)),
                pl.BlockSpec((n_cols, FEAT), lambda i, where: (0, 0)),
            ],
            out_specs=pl.BlockSpec((TILE_R, n_cols), lambda i, where: (i, 0)),
            scratch_shapes=[
                pltpu.VMEM((n_cols, FEAT), jnp.bfloat16),
                pltpu.VMEM((2, TILE_R, TILE_C), jnp.float32),
                pltpu.VMEM((n_cols // TILE_C, 8, TILE_C), jnp.float32),
                pltpu.VMEM((n_cols // TILE_C, 8, TILE_C), jnp.float32),
                pltpu.VMEM((TILE_R, 128), jnp.float32),
                pltpu.VMEM((TILE_R, 128), jnp.float32),
            ],
        ),
        name="tiles",
        cost_estimate=pl.CostEstimate(flops=int(30e9), bytes_accessed=int(12e6), transcendentals=0),
    )(where, near, far, cols)


def solve(x, v_ref):
    hi, lo = split(x)
    parts = []
    for n in range(4):
        depth = n * 128 + 128
        v_hi = v_ref[:depth, n * 128 : depth]
        v_lo = v_ref[:depth, PANEL + n * 128 : PANEL + depth]
        dot = functools.partial(jnp.dot, preferred_element_type=jnp.float32)
        parts.append(dot(hi[:, :depth], v_hi) + dot(hi[:, :depth], v_lo) + dot(lo[:, :depth], v_hi))
    return jnp.concatenate(parts, axis=1)


def update_kernel(where_ref, kernel_ref, near_ref, far_ref, cols_ref, v_ref, out_ref, hi_c, lo_c, left):
    step = pl.program_id(0)
    row_index = where_ref[0]
    col_index = where_ref[1]
    count = cols_ref.shape[0] // TILE_C

    @pl.when(step == 0)
    def _():
        def body(t, carry):
            rows = pl.ds(pl.multiple_of(t * TILE_C, TILE_C), TILE_C)
            hi, lo = split(solve(in_order(cols_ref[rows, :]), v_ref))
            hi_c[rows, :] = hi
            lo_c[rows, :] = lo
            return carry

        lax.fori_loop(0, count, body, 0)

    _, other = slot_of(step, where_ref)
    solved = solve(jnp.where(other == 1, far_ref[0], near_ref[0]), v_ref)
    hi_r, lo_r = split(solved)
    for n in range(4):
        left[n] = solved[:, n * 128 : n * 128 + 128]

    def masked(value, t):
        s = lax.broadcasted_iota(jnp.int32, (TILE_R, TILE_C), 0)
        v = lax.broadcasted_iota(jnp.int32, (TILE_R, TILE_C), 1)
        row_id = (step * 4 + s // 32) * PANEL + row_index * 32 + s % 32
        col_id = (t * 4 + v // 64) * PANEL + col_index * 64 + v % 64
        return jnp.where(row_id >= col_id, value, 0.0)

    for t in range(count):
        lanes = slice(t * TILE_C, t * TILE_C + TILE_C)

        @pl.when(step < t)
        def _():
            out_ref[:, lanes] = jnp.zeros((TILE_R, TILE_C), jnp.float32)

        @pl.when(step >= t)
        def _():
            drop = (
                dot_nt(hi_r, hi_c[lanes, :])
                + dot_nt(hi_r, lo_c[lanes, :])
                + dot_nt(lo_r, hi_c[lanes, :])
            )
            value = kernel_ref[:, lanes] - drop
            if t == 0:
                mine = left[col_index // 2]
                mine = jnp.where(col_index % 2 == 1, pltpu.roll(mine, 64, 1), mine)
                mine = jnp.concatenate([mine, mine], axis=1)
                v = lax.broadcasted_iota(jnp.int32, (TILE_R, TILE_C), 1)
                value = jnp.where(v < 64, mine, value)
            out_ref[:, lanes] = value

            @pl.when(step == t)
            def _():
                out_ref[:, lanes] = masked(out_ref[:, lanes], t)


def update(where, kernel, near, far, cols, v):
    n_rows, n_cols = kernel.shape
    piece = (1, TILE_R, PANEL)
    return pl.pallas_call(
        update_kernel,
        out_shape=jax.ShapeDtypeStruct((n_rows, n_cols), jnp.float32),
        grid_spec=pltpu.PrefetchScalarGridSpec(
            num_scalar_prefetch=1,
            grid=(n_rows // TILE_R,),
            in_specs=[
                pl.BlockSpec((TILE_R, n_cols), lambda i, where: (i, 0)),
                pl.BlockSpec(piece, lambda i, where: (slot_of(i, where)[0], 0, 0)),
                pl.BlockSpec(piece, lambda i, where: (slot_of(i, where)[0], 0, 0)),
                pl.BlockSpec((n_cols, PANEL), lambda i, where: (0, 0)),
                pl.BlockSpec((PANEL, 2 * PANEL), lambda i, where: (0, 0)),
            ],
            out_specs=pl.BlockSpec((TILE_R, n_cols), lambda i, where: (i, 0)),
            scratch_shapes=[
                pltpu.VMEM((n_cols, PANEL), jnp.bfloat16),
                pltpu.VMEM((n_cols, PANEL), jnp.bfloat16),
                pltpu.VMEM((4, TILE_R, 128), jnp.float32),
            ],
        ),
        name="update",
        cost_estimate=pl.CostEstimate(flops=int(6e9), bytes_accessed=int(20e6), transcendentals=0),
    )(where, kernel, near, far, cols, v)


def send(x, target):
    pairs = [(r * 8 + k, target(r, k)) for r in range(16) for k in range(8)]
    return lax.ppermute(x, ("row", "col"), [(s, t[0] * 8 + t[1]) for s, t in pairs if t])


def along_z(d):
    return lambda r, k: (r, (k + 2 * d) % 8)


def along_y(d):
    return lambda r, k: ((r + 4 * d) % 16, k)


def along_x(d):
    return lambda r, k: (r // 4 * 4 + (r + d) % 4, k)


def other_core(r, k):
    return r, k ^ 1


def to_columns(x):
    moved = send(x, lambda r, k: (k * 2 + r % 2, r // 2))
    return lax.all_gather(moved, "row", axis=0, tiled=True)


def to_rows(x):
    near = jnp.stack([x] + [send(x, along_z(d)) for d in (1, 2, 3)])
    return near, send(near, other_core)


def to_all(x):
    head = jnp.where(lax.axis_index("col") == 0, x[:32], jnp.zeros((32, FEAT), x.dtype))
    for bit in (1, 2, 4):
        head = head + send(head, lambda r, k: (r, k | bit) if k < bit else None)
    column = jnp.stack([head] + [send(head, along_y(d)) for d in (1, 2, 3)])
    return [column] + [send(column, along_x(d)) for d in (1, 2, 3)]


def per_device(samples):
    where = jnp.stack([lax.axis_index("row"), lax.axis_index("col")]).astype(jnp.int32)
    pieces = to_all(samples)
    if WAIT:
        samples_later, pieces = lax.optimization_barrier((samples, pieces))
    else:
        samples_later = samples
    corner, own = leading(where, pieces, samples)
    col_feats = to_columns(samples_later)
    own_cols = to_columns(own)
    near_feats, far_feats = to_rows(samples_later)
    near, far = to_rows(own)
    v = factor(corner)
    kernel = tiles(where, near_feats, far_feats, col_feats)
    return update(where, kernel, near, far, own_cols, v)


WAIT = True


def solution(mesh):
    return jax.shard_map(
        per_device,
        mesh=mesh,
        in_specs=(P(("row", "col"), None),),
        out_specs=P("row", "col"),
        check_vma=False,
    )
```

time: 223 us -> 228 us (1.022)
  blocking collectives: 44.7 us -> 0 us
  starting transfers between devices: 14.2 us -> 54 us
  waiting for transfers between devices: 21 us -> 28.5 us
    all_gather x2 -> x0, blocking collectives: 44.7 us -> none  [the longest x1 23.5 us: per_device(): head = lax.all_gather(samples[:PANEL // row_count], 'col', axis=0)[0]]
    ppermute x2 -> x19, starting transfers between devices: 14.1 us -> 54 us  [send(): lax.ppermute(x, ('row', 'col'), [(s, t[0] * 8 + t[1]) for s, t in pairs i...]
    ppermute x2 -> x19, waiting for transfers between devices: 7.8 us -> 28.4 us  [send(): lax.ppermute(x, ('row', 'col'), [(s, t[0] * 8 + t[1]) for s, t in pairs i...]
    all_gather x2, waiting for transfers between devices: 12.4 us -> 0.02 us  [to_columns(): return lax.all_gather(moved, 'row', axis=0, tiled=True)]
    pallas_call x1, Pallas kernels: 57.6 us -> 46.2 us  [tiles(): pl.pallas_call(tiles_kernel, out_shape=jax.ShapeDtypeStruct((n_rows, n_co...]
    pallas_call x1, Pallas kernels: 19.2 us -> 29.3 us  [update(): pl.pallas_call(update_kernel, out_shape=jax.ShapeDtypeStruct((n_rows, n_c...]
    pallas_call x1 -> x2, Pallas kernels: 49.8 us -> 50.2 us  [the longest x1 38.6 us: factor(): pl.pallas_call(factor_kernel, out_shape=jax.ShapeDtypeStruct((PANEL, 2 *...]
  transfers between devices with their start and end apart: 6 -> 21, of which waited for: 3 -> 13; matrix products, arithmetic and copies ran while one was open for 1% -> 0% of each run, Pallas kernels for 48% -> 43%
where the time goes in v2:
time: 228 us; the launch traced here: 227 us
  Pallas kernels  126 us (55%)
  starting transfers between devices  54 us (24%)
  waiting for transfers between devices  28.5 us (12%)
  between operations  13.6 us (6%)
  other arithmetic  2.43 us (1%)
  local copies, waits for them, and re-layouts  2.36 us (1%)
    ppermute x19, starting transfers between devices, send(): lax.ppermute(x, ('row', 'col'), [(s, t[0] * 8 + t[1]) for s, t in pairs i...  54 us
    pallas_call x1, Pallas kernels, tiles(): pl.pallas_call(tiles_kernel, out_shape=jax.ShapeDtypeStruct((n_rows, n_co...  46.2 us
    pallas_call x1, Pallas kernels, factor(): pl.pallas_call(factor_kernel, out_shape=jax.ShapeDtypeStruct((PANEL, 2 *...  38.6 us
    pallas_call x1, Pallas kernels, update(): pl.pallas_call(update_kernel, out_shape=jax.ShapeDtypeStruct((n_rows, n_c...  29.3 us
    ppermute x19, waiting for transfers between devices, send(): lax.ppermute(x, ('row', 'col'), [(s, t[0] * 8 + t[1]) for s, t in pairs i...  28.4 us
    pallas_call x1, Pallas kernels, leading(): pl.pallas_call(leading_kernel, out_shape=(jax.ShapeDtypeStruct((PANEL, PA...  11.6 us
  transfers between devices with their start and end apart: 21, of which 13 were waited for; matrix products, arithmetic and copies ran while one was open for 0% of the time, Pallas kernels for 43%

profile of v2, /device:TPU:1, one launch (start us, length us, event | category | flops | bytes accessed | tf_op | source)
XLA Modules:
  0.0 226.6 jit_solution(5453598938908688957)
XLA Ops:
  7.3 1.3 collective-permute-start
  8.6 2.1 collective-permute-done
  11.5 1.7 collective-permute-start.1
  13.2 1.2 collective-permute-done.1
  14.4 1.5 collective-permute-start.2
  15.8 1.2 collective-permute-done.2
  17.0 2.8 %collective-permute-start.5 = (bf16[32,768]{1,0:T(8,128)(2,1)S(1)}, bf16[32,768]{1,0:T(8,128)(2,1)S(1)}, u32[]{:S(2)}, u32[]{:S(2)}) collective-permute-start(bf16[32,768]{1,0:T(8,128)(2,1)S(1)} %add.11), channel_id=1, source_target_pairs={{0,96},{1,97},{2,98},{3,99},{4,100},{5,101},{6,102},{7,103},{8,104... | collective-permute-start | bytes 147464 | tf_op jit(solution)/shard_map/ppermute | solution.py:475
  21.0 3.3 %collective-permute-done.4 = bf16[32,768]{1,0:T(8,128)(2,1)S(1)} collective-permute-done((bf16[32,768]{1,0:T(8,128)(2,1)S(1)}, bf16[32,768]{1,0:T(8,128)(2,1)S(1)}, u32[]{:S(2)}, u32[]{:S(2)}) %collective-permute-start.4) | collective-permute-done | bytes 49184 | tf_op jit(solution)/shard_map/ppermute | solution.py:475
  24.8 2.5 %collective-permute-start.8 = (bf16[4,32,768]{2,1,0:T(8,128)(2,1)S(1)}, bf16[4,32,768]{2,1,0:T(8,128)(2,1)S(1)}, u32[]{:S(2)}, u32[]{:S(2)}) collective-permute-start(bf16[4,32,768]{2,1,0:T(8,128)(2,1)S(1)} %pad_maximum_fusion.2.g0), channel_id=1, source_target_pairs={{0,24},{1,25},{2,26},{3,27},{4,28},{5,29},{6,30},{7,31},{8,0},{9,1... | collective-permute-start | bytes 589832 | tf_op jit(solution)/shard_map/ppermute | solution.py:475
  28.5 3.9 %collective-permute-done.8.g3 = bf16[4,32,768]{2,1,0:T(8,128)(2,1)S(1)} collective-permute-done((bf16[4,32,768]{2,1,0:T(8,128)(2,1)S(1)}, bf16[4,32,768]{2,1,0:T(8,128)(2,1)S(1)}, u32[]{:S(2)}, u32[]{:S(2)}) %collective-permute-start.8) | collective-permute-done | bytes 196640 | tf_op jit(solution)/shard_map/ppermute | solution.py:475
  33.5 2.4 %collective-permute-done.6.g1 = bf16[4,32,768]{2,1,0:T(8,128)(2,1)S(1)} collective-permute-done((bf16[4,32,768]{2,1,0:T(8,128)(2,1)S(1)}, bf16[4,32,768]{2,1,0:T(8,128)(2,1)S(1)}, u32[]{:S(2)}, u32[]{:S(2)}) %collective-permute-start.6) | collective-permute-done | bytes 196640 | tf_op jit(solution)/shard_map/ppermute | solution.py:475
  35.9 6.8 %collective-permute-start.13 = (bf16[128,768]{1,0:T(8,128)(2,1)}, bf16[128,768]{1,0:T(8,128)(2,1)S(1)}, u32[]{:S(2)}, u32[]{:S(2)}) collective-permute-start(bf16[128,768]{1,0:T(8,128)(2,1)} %own_ref.1), channel_id=1, source_target_pairs={{0,0},{1,16},{2,32},{3,48},{4,64},{5,80},{6,96},{7,112},{8,8},{9,2... | collective-permute-start | bytes 589832 | tf_op jit(solution)/shard_map/ppermute | solution.py:475
  42.7 3.5 %collective-permute-done.13 = bf16[128,768]{1,0:T(8,128)(2,1)S(1)} collective-permute-done((bf16[128,768]{1,0:T(8,128)(2,1)}, bf16[128,768]{1,0:T(8,128)(2,1)S(1)}, u32[]{:S(2)}, u32[]{:S(2)}) %collective-permute-start.13) | collective-permute-done | bytes 196640 | tf_op jit(solution)/shard_map/ppermute | solution.py:475
  47.7 11.6 %leading.1 = (f32[512,512]{1,0:T(8,128)}, f32[128,512]{1,0:T(8,128)}) custom-call(s32[2]{0:T(128)} %pad_add_fusion.where_ref, bf16[4,32,768]{2,1,0:T(8,128)(2,1)} %copy-done.7, bf16[4,32,768]{2,1,0:T(8,128)(2,1)} %copy-done.10, bf16[4,32,768]{2,1,0:T(8,128)(2,1)} %copy-done.9, bf16[4,32,768]{2,1,0:T(8,128)(2,1)} %copy-done.8, bf16[128,768]{1,0:T(8,128)(2,1)} %own_ref.1), custom_call_target="tpu_custom_call" | custom-call | flops 8000000000 | bytes 2000000 | tf_op jit(solution)/shard_map/leading/pallas_call | solution.py:165
  59.2 5.1 %collective-permute-start.18 = (f32[128,512]{1,0:T(8,128)}, f32[128,512]{1,0:T(8,128)S(1)}, u32[]{:S(2)}, u32[]{:S(2)}) collective-permute-start(f32[128,512]{1,0:T(8,128)} %get-tuple-element.17), channel_id=1, source_target_pairs={{0,0},{1,16},{2,32},{3,48},{4,64},{5,80},{6,96},{7,112},{8,8},{9,2... | collective-permute-start | bytes 786440 | tf_op jit(solution)/shard_map/ppermute | solution.py:475
  64.4 5.4 %collective-permute-done.18 = f32[128,512]{1,0:T(8,128)S(1)} collective-permute-done((f32[128,512]{1,0:T(8,128)}, f32[128,512]{1,0:T(8,128)S(1)}, u32[]{:S(2)}, u32[]{:S(2)}) %collective-permute-start.18) | collective-permute-done | bytes 262176 | tf_op jit(solution)/shard_map/ppermute | solution.py:475
  70.6 13.8 %collective-permute-start.11 = (bf16[128,768]{1,0:T(8,128)(2,1)S(1)}, bf16[128,768]{1,0:T(8,128)(2,1)S(1)}, u32[]{:S(2)}, u32[]{:S(2)}) collective-permute-start(bf16[128,768]{1,0:T(8,128)(2,1)S(1)} %copy-done.3), channel_id=1, source_target_pairs={{0,6},{1,7},{2,0},{3,1},{4,2},{5,3},{6,4},{7,5},{8,14},{9,15},{10,... | collective-permute-start | bytes 589832 | tf_op jit(solution)/shard_map/ppermute | solution.py:475
  85.8 1.9 collective-permute-start.16
  88.8 1.9 collective-permute-done.11
  90.7 1.8 collective-permute-done.9
  92.6 11.5 %collective-permute-start.12 = (bf16[4,128,768]{2,1,0:T(8,128)(2,1)S(1)}, bf16[4,128,768]{2,1,0:T(8,128)(2,1)}, u32[]{:S(2)}, u32[]{:S(2)}) collective-permute-start(bf16[4,128,768]{2,1,0:T(8,128)(2,1)S(1)} %pad_maximum_fusion.1.near_ref), channel_id=1, source_target_pairs={{0,1},{1,0},{2,3},{3,2},{4,5},{5,4},{6,7},{7,6},{8,9},{9,8},{10,11... | collective-permute-start | bytes 2359304 | tf_op jit(solution)/shard_map/ppermute | solution.py:475
  104.2 38.6 %factor.1.v_ref = bf16[512,1024]{1,0:T(8,128)(2,1)} custom-call(f32[512,512]{1,0:T(8,128)} %get-tuple-element.18.corner_ref), custom_call_target="tpu_custom_call" | custom-call | flops 24999999488 | bytes 2000000 | tf_op jit(solution)/shard_map/factor/pallas_call | solution.py:260
  143.2 46.2 %tiles.1.kernel_ref = f32[1024,2048]{1,0:T(8,128)} custom-call(s32[2]{0:T(128)} %pad_add_fusion.where_ref, bf16[4,128,768]{2,1,0:T(8,128)(2,1)} %copy-done.2, bf16[4,128,768]{2,1,0:T(8,128)(2,1)} %collective-permute-done.12.far_ref, bf16[2048,768]{1,0:T(8,128)(2,1)} %all-gather.3.cloned.1.call-done.cols_ref), custom_call_target="tpu_custom_call" | custom-call | flops 30000001024 | bytes 12000000 | tf_op jit(solution)/shard_map/tiles/pallas_call | solution.py:349
  190.5 29.3 %update.1 = f32[1024,2048]{1,0:T(8,128)} custom-call(s32[2]{0:T(128)} %pad_add_fusion.where_ref, f32[1024,2048]{1,0:T(8,128)} %tiles.1.kernel_ref, f32[4,128,512]{2,1,0:T(8,128)} %copy-done, f32[4,128,512]{2,1,0:T(8,128)} %copy-done.1, f32[2048,512]{1,0:T(8,128)} %all-gather.5.cloned.1.call-done.cols_ref, bf16[512,1024]{1,0:T(8,128)(2,1)} %factor.1.v_ref), custom_call_target="tpu_custom_call" | custom-call | flops 6000000000 | bytes 20000000 | tf_op jit(solution)/shard_map/update/pallas_call | solution.py:448
  (54 shorter events, 11.7 us)
Async XLA Ops:
  6.5 136.7 %all-gather.3.cloned.1.call-start = ((), (), s32[]{:S(2)}) async-start(), calls=%async_computation | async-start | bytes 3342336 | tf_op jit(solution)/shard_map/all_gather | solution.py:496
  7.3 3.4 %collective-permute-start = (bf16[32,768]{1,0:T(8,128)(2,1)S(1)}, bf16[32,768]{1,0:T(8,128)(2,1)S(1)}, u32[]{:S(2)}, u32[]{:S(2)}) collective-permute-start(bf16[32,768]{1,0:T(8,128)(2,1)S(1)} %slice_select_fusion), channel_id=1, source_target_pairs={{0,1},{8,9},{16,17},{24,25},{32,33},{40,41},{48,49},{56,57},{64,65... | collective-permute-start | bytes 147464 | tf_op jit(solution)/shard_map/ppermute | solution.py:475
  11.5 2.8 %collective-permute-start.1 = (bf16[32,768]{1,0:T(8,128)(2,1)S(1)}, bf16[32,768]{1,0:T(8,128)(2,1)S(1)}, u32[]{:S(2)}, u32[]{:S(2)}) collective-permute-start(bf16[32,768]{1,0:T(8,128)(2,1)S(1)} %fusion), channel_id=1, source_target_pairs={{0,2},{1,3},{8,10},{9,11},{16,18},{17,19},{24,26},{25,27},{32,34},... | collective-permute-start | bytes 147464 | tf_op jit(solution)/shard_map/ppermute | solution.py:475
  14.4 2.6 %collective-permute-start.2 = (bf16[32,768]{1,0:T(8,128)(2,1)S(1)}, bf16[32,768]{1,0:T(8,128)(2,1)S(1)}, u32[]{:S(2)}, u32[]{:S(2)}) collective-permute-start(bf16[32,768]{1,0:T(8,128)(2,1)S(1)} %add.10), channel_id=1, source_target_pairs={{0,4},{1,5},{2,6},{3,7},{8,12},{9,13},{10,14},{11,15},{16,20},{17,... | collective-permute-start | bytes 147464 | tf_op jit(solution)/shard_map/ppermute | solution.py:475
  17.0 4.0 %collective-permute-start.5 = (bf16[32,768]{1,0:T(8,128)(2,1)S(1)}, bf16[32,768]{1,0:T(8,128)(2,1)S(1)}, u32[]{:S(2)}, u32[]{:S(2)}) collective-permute-start(bf16[32,768]{1,0:T(8,128)(2,1)S(1)} %add.11), channel_id=1, source_target_pairs={{0,96},{1,97},{2,98},{3,99},{4,100},{5,101},{6,102},{7,103},{8,104... | collective-permute-start | bytes 147464 | tf_op jit(solution)/shard_map/ppermute | solution.py:475
  19.8 4.5 %collective-permute-start.4 = (bf16[32,768]{1,0:T(8,128)(2,1)S(1)}, bf16[32,768]{1,0:T(8,128)(2,1)S(1)}, u32[]{:S(2)}, u32[]{:S(2)}) collective-permute-start(bf16[32,768]{1,0:T(8,128)(2,1)S(1)} %add.11), channel_id=1, source_target_pairs={{0,64},{1,65},{2,66},{3,67},{4,68},{5,69},{6,70},{7,71},{8,72},{9,... | collective-permute-start | bytes 147464 | tf_op jit(solution)/shard_map/ppermute | solution.py:475
  20.2 4.6 %collective-permute-start.3 = (bf16[32,768]{1,0:T(8,128)(2,1)S(1)}, bf16[32,768]{1,0:T(8,128)(2,1)S(1)}, u32[]{:S(2)}, u32[]{:S(2)}) collective-permute-start(bf16[32,768]{1,0:T(8,128)(2,1)S(1)} %add.11), channel_id=1, source_target_pairs={{0,32},{1,33},{2,34},{3,35},{4,36},{5,37},{6,38},{7,39},{8,40},{9,... | collective-permute-start | bytes 147464 | tf_op jit(solution)/shard_map/ppermute | solution.py:475
  24.8 7.5 %collective-permute-start.8 = (bf16[4,32,768]{2,1,0:T(8,128)(2,1)S(1)}, bf16[4,32,768]{2,1,0:T(8,128)(2,1)S(1)}, u32[]{:S(2)}, u32[]{:S(2)}) collective-permute-start(bf16[4,32,768]{2,1,0:T(8,128)(2,1)S(1)} %pad_maximum_fusion.2.g0), channel_id=1, source_target_pairs={{0,24},{1,25},{2,26},{3,27},{4,28},{5,29},{6,30},{7,31},{8,0},{9,1... | collective-permute-start | bytes 589832 | tf_op jit(solution)/shard_map/ppermute | solution.py:475
  27.4 6.1 %collective-permute-start.7 = (bf16[4,32,768]{2,1,0:T(8,128)(2,1)S(1)}, bf16[4,32,768]{2,1,0:T(8,128)(2,1)S(1)}, u32[]{:S(2)}, u32[]{:S(2)}) collective-permute-start(bf16[4,32,768]{2,1,0:T(8,128)(2,1)S(1)} %pad_maximum_fusion.2.g0), channel_id=1, source_target_pairs={{0,16},{1,17},{2,18},{3,19},{4,20},{5,21},{6,22},{7,23},{8,24},{9,... | collective-permute-start | bytes 589832 | tf_op jit(solution)/shard_map/ppermute | solution.py:475
  27.9 8.0 %collective-permute-start.6 = (bf16[4,32,768]{2,1,0:T(8,128)(2,1)S(1)}, bf16[4,32,768]{2,1,0:T(8,128)(2,1)S(1)}, u32[]{:S(2)}, u32[]{:S(2)}) collective-permute-start(bf16[4,32,768]{2,1,0:T(8,128)(2,1)S(1)} %pad_maximum_fusion.2.g0), channel_id=1, source_target_pairs={{0,8},{1,9},{2,10},{3,11},{4,12},{5,13},{6,14},{7,15},{8,16},{9,17... | collective-permute-start | bytes 589832 | tf_op jit(solution)/shard_map/ppermute | solution.py:475
  35.9 10.3 %collective-permute-start.13 = (bf16[128,768]{1,0:T(8,128)(2,1)}, bf16[128,768]{1,0:T(8,128)(2,1)S(1)}, u32[]{:S(2)}, u32[]{:S(2)}) collective-permute-start(bf16[128,768]{1,0:T(8,128)(2,1)} %own_ref.1), channel_id=1, source_target_pairs={{0,0},{1,16},{2,32},{3,48},{4,64},{5,80},{6,96},{7,112},{8,8},{9,2... | collective-permute-start | bytes 589832 | tf_op jit(solution)/shard_map/ppermute | solution.py:475
  47.0 142.5 %all-gather.5.cloned.1.call-start = ((), (), s32[]{:S(2)}) async-start(), calls=%async_computation.1 | async-start | bytes 4456448 | tf_op jit(solution)/shard_map/all_gather | solution.py:496
  59.2 10.6 %collective-permute-start.18 = (f32[128,512]{1,0:T(8,128)}, f32[128,512]{1,0:T(8,128)S(1)}, u32[]{:S(2)}, u32[]{:S(2)}) collective-permute-start(f32[128,512]{1,0:T(8,128)} %get-tuple-element.17), channel_id=1, source_target_pairs={{0,0},{1,16},{2,32},{3,48},{4,64},{5,80},{6,96},{7,112},{8,8},{9,2... | collective-permute-start | bytes 786440 | tf_op jit(solution)/shard_map/ppermute | solution.py:475
  70.6 20.1 %collective-permute-start.11 = (bf16[128,768]{1,0:T(8,128)(2,1)S(1)}, bf16[128,768]{1,0:T(8,128)(2,1)S(1)}, u32[]{:S(2)}, u32[]{:S(2)}) collective-permute-start(bf16[128,768]{1,0:T(8,128)(2,1)S(1)} %copy-done.3), channel_id=1, source_target_pairs={{0,6},{1,7},{2,0},{3,1},{4,2},{5,3},{6,4},{7,5},{8,14},{9,15},{10,... | collective-permute-start | bytes 589832 | tf_op jit(solution)/shard_map/ppermute | solution.py:475
  84.4 6.3 %collective-permute-start.10 = (bf16[128,768]{1,0:T(8,128)(2,1)S(1)}, bf16[128,768]{1,0:T(8,128)(2,1)S(1)}, u32[]{:S(2)}, u32[]{:S(2)}) collective-permute-start(bf16[128,768]{1,0:T(8,128)(2,1)S(1)} %copy-done.3), channel_id=1, source_target_pairs={{0,4},{1,5},{2,6},{3,7},{4,0},{5,1},{6,2},{7,3},{8,12},{9,13},{10,... | collective-permute-start | bytes 589832 | tf_op jit(solution)/shard_map/ppermute | solution.py:475
  85.1 7.5 %collective-permute-start.9 = (bf16[128,768]{1,0:T(8,128)(2,1)S(1)}, bf16[128,768]{1,0:T(8,128)(2,1)S(1)}, u32[]{:S(2)}, u32[]{:S(2)}) collective-permute-start(bf16[128,768]{1,0:T(8,128)(2,1)S(1)} %copy-done.3), channel_id=1, source_target_pairs={{0,2},{1,3},{2,4},{3,5},{4,6},{5,7},{6,0},{7,1},{8,10},{9,11},{10,... | collective-permute-start | bytes 589832 | tf_op jit(solution)/shard_map/ppermute | solution.py:475
  85.8 56.9 %collective-permute-start.16 = (f32[128,512]{1,0:T(8,128)}, f32[128,512]{1,0:T(8,128)S(1)}, u32[]{:S(2)}, u32[]{:S(2)}) collective-permute-start(f32[128,512]{1,0:T(8,128)} %get-tuple-element.17), channel_id=1, source_target_pairs={{0,6},{1,7},{2,0},{3,1},{4,2},{5,3},{6,4},{7,5},{8,14},{9,15},{10,... | collective-permute-start | bytes 786440 | tf_op jit(solution)/shard_map/ppermute | solution.py:475
  87.7 55.0 %collective-permute-start.15 = (f32[128,512]{1,0:T(8,128)}, f32[128,512]{1,0:T(8,128)S(1)}, u32[]{:S(2)}, u32[]{:S(2)}) collective-permute-start(f32[128,512]{1,0:T(8,128)} %get-tuple-element.17), channel_id=1, source_target_pairs={{0,4},{1,5},{2,6},{3,7},{4,0},{5,1},{6,2},{7,3},{8,12},{9,13},{10,... | collective-permute-start | bytes 786440 | tf_op jit(solution)/shard_map/ppermute | solution.py:475
  90.7 52.0 %collective-permute-start.14 = (f32[128,512]{1,0:T(8,128)}, f32[128,512]{1,0:T(8,128)S(1)}, u32[]{:S(2)}, u32[]{:S(2)}) collective-permute-start(f32[128,512]{1,0:T(8,128)} %get-tuple-element.17), channel_id=1, source_target_pairs={{0,2},{1,3},{2,4},{3,5},{4,6},{5,7},{6,0},{7,1},{8,10},{9,11},{10,... | collective-permute-start | bytes 786440 | tf_op jit(solution)/shard_map/ppermute | solution.py:475
  92.6 50.1 %copy-start.2 = (bf16[4,128,768]{2,1,0:T(8,128)(2,1)}, bf16[4,128,768]{2,1,0:T(8,128)(2,1)S(1)}, u32[]{:S(2)}) copy-start(bf16[4,128,768]{2,1,0:T(8,128)(2,1)S(1)} %pad_maximum_fusion.1.near_ref) | copy-start | bytes 2359300
  92.6 50.6 %collective-permute-start.12 = (bf16[4,128,768]{2,1,0:T(8,128)(2,1)S(1)}, bf16[4,128,768]{2,1,0:T(8,128)(2,1)}, u32[]{:S(2)}, u32[]{:S(2)}) collective-permute-start(bf16[4,128,768]{2,1,0:T(8,128)(2,1)S(1)} %pad_maximum_fusion.1.near_ref), channel_id=1, source_target_pairs={{0,1},{1,0},{2,3},{3,2},{4,5},{5,4},{6,7},{7,6},{8,9},{9,8},{10,11... | collective-permute-start | bytes 2359304 | tf_op jit(solution)/shard_map/ppermute | solution.py:475
  104.2 38.6 %copy-start.5 = (f32[128,512]{1,0:T(8,128)S(1)}, f32[128,512]{1,0:T(8,128)}, u32[]{:S(2)}) copy-start(f32[128,512]{1,0:T(8,128)} %get-tuple-element.17) | copy-start | bytes 786436
  142.8 46.6 %copy-start = (f32[4,128,512]{2,1,0:T(8,128)}, f32[4,128,512]{2,1,0:T(8,128)S(1)}, u32[]{:S(2)}) copy-start(f32[4,128,512]{2,1,0:T(8,128)S(1)} %pad_maximum_fusion.near_ref) | copy-start | bytes 3145732
  142.9 46.6 %collective-permute-start.17 = (f32[4,128,512]{2,1,0:T(8,128)S(1)}, f32[4,128,512]{2,1,0:T(8,128)S(1)}, u32[]{:S(2)}, u32[]{:S(2)}) collective-permute-start(f32[4,128,512]{2,1,0:T(8,128)S(1)} %pad_maximum_fusion.near_ref), channel_id=1, source_target_pairs={{0,1},{1,0},{2,3},{3,2},{4,5},{5,4},{6,7},{7,6},{8,9},{9,8},{10,11... | collective-permute-start | bytes 3145736 | tf_op jit(solution)/shard_map/ppermute | solution.py:475
  (8 other events, 89.2 us)
Sparse Core Ops, SparseCore 0:
  47.1 60.4 all-gather.2
  109.7 50.6 all-gather.4

commit v3 on v2

--- a/solution.py
+++ b/solution.py
@@ -272,7 +272,7 @@
 
 
 def tiles_kernel(
-    where_ref, near_ref, far_ref, cols_ref, out_ref, cols, gram, inv_ac, scl_ac, inv_dn, scl_dn
+    where_ref, rows_ref, cols_ref, out_ref, cols, gram, inv_ac, scl_ac, inv_dn, scl_dn
 ):
     step = pl.program_id(0)
     row_index = where_ref[0]
@@ -293,8 +293,7 @@
 
         lax.fori_loop(0, count, body, 0)
 
-    _, other = slot_of(step, where_ref)
-    x = jnp.where(other == 1, far_ref[0], near_ref[0])
+    x = rows_ref[...]
     n = norms_down(x)
     r = lax.rsqrt(n)
     inv_dn[...] = r
@@ -343,9 +342,8 @@
             out_ref[rows, pl.ds(first, 128)] = value
 
 
-def tiles(where, near, far, cols):
-    n_rows, n_cols = 8 * TILE_R, cols.shape[0]
-    piece = (1, TILE_R, FEAT)
+def tiles(where, rows, cols):
+    n_rows, n_cols = rows.shape[0], cols.shape[0]
     return pl.pallas_call(
         tiles_kernel,
         out_shape=jax.ShapeDtypeStruct((n_rows, n_cols), jnp.float32),
@@ -353,8 +351,7 @@
             num_scalar_prefetch=1,
             grid=(n_rows // TILE_R,),
             in_specs=[
-                pl.BlockSpec(piece, lambda i, where: (slot_of(i, where)[0], 0, 0)),
-                pl.BlockSpec(piece, lambda i, where: (slot_of(i, where)[0], 0, 0)),
+                pl.BlockSpec((TILE_R, FEAT), lambda i, where: (i, 0)),
                 pl.BlockSpec((n_cols, FEAT), lambda i, where: (0, 0)),
             ],
             out_specs=pl.BlockSpec((TILE_R, n_cols), lambda i, where: (i, 0)),
@@ -369,22 +366,24 @@
         ),
         name="tiles",
         cost_estimate=pl.CostEstimate(flops=int(30e9), bytes_accessed=int(12e6), transcendentals=0),
-    )(where, near, far, cols)
+    )(where, rows, cols)
 
 
 def solve(x, v_ref):
     hi, lo = split(x)
     parts = []
-    for n in range(4):
-        depth = n * 128 + 128
-        v_hi = v_ref[:depth, n * 128 : depth]
-        v_lo = v_ref[:depth, PANEL + n * 128 : PANEL + depth]
-        dot = functools.partial(jnp.dot, preferred_element_type=jnp.float32)
-        parts.append(dot(hi[:, :depth], v_hi) + dot(hi[:, :depth], v_lo) + dot(lo[:, :depth], v_hi))
+    for start in range(0, PANEL, 256):
+        depth = start + 256
+        v_hi = v_ref[:depth, start:depth]
+        v_lo = v_ref[:depth, PANEL + start : PANEL + depth]
+        left = jnp.concatenate([hi[:, :depth], hi[:, :depth], lo[:, :depth]], axis=1)
+        right = jnp.concatenate([v_hi, v_lo, v_hi], axis=0)
+        parts.append(jnp.dot(left, right, preferred_element_type=jnp.float32))
     return jnp.concatenate(parts, axis=1)
 
 
-def update_kernel(where_ref, kernel_ref, near_ref, far_ref, cols_ref, v_ref, out_ref, hi_c, lo_c, left):
+def update_kernel(where_ref, kernel_ref, *refs):
+    near_refs, (cols_ref, v_ref, out_ref, both_c, left) = refs[:4], refs[4:]
     step = pl.program_id(0)
     row_index = where_ref[0]
     col_index = where_ref[1]
@@ -395,79 +394,79 @@
         def body(t, carry):
             rows = pl.ds(pl.multiple_of(t * TILE_C, TILE_C), TILE_C)
             hi, lo = split(solve(in_order(cols_ref[rows, :]), v_ref))
-            hi_c[rows, :] = hi
-            lo_c[rows, :] = lo
+            both_c[rows, :PANEL] = hi
+            both_c[rows, PANEL:] = lo
             return carry
 
         lax.fori_loop(0, count, body, 0)
 
-    _, other = slot_of(step, where_ref)
-    solved = solve(jnp.where(other == 1, far_ref[0], near_ref[0]), v_ref)
+    pieces = []
+    for half in range(2):
+        _, other = slot_of(step * 2 + half, where_ref)
+        pieces.append(jnp.where(other == 1, near_refs[2 * half + 1][0], near_refs[2 * half][0]))
+    solved = solve(jnp.concatenate(pieces, axis=0), v_ref)
     hi_r, lo_r = split(solved)
+    all_r = jnp.concatenate([hi_r, hi_r, lo_r], axis=1)
     for n in range(4):
         left[n] = solved[:, n * 128 : n * 128 + 128]
-
-    def masked(value, t):
-        s = lax.broadcasted_iota(jnp.int32, (TILE_R, TILE_C), 0)
-        v = lax.broadcasted_iota(jnp.int32, (TILE_R, TILE_C), 1)
-        row_id = (step * 4 + s // 32) * PANEL + row_index * 32 + s % 32
-        col_id = (t * 4 + v // 64) * PANEL + col_index * 64 + v % 64
-        return jnp.where(row_id >= col_id, value, 0.0)
+    tall = 2 * TILE_R
 
     for t in range(count):
         lanes = slice(t * TILE_C, t * TILE_C + TILE_C)
 
-        @pl.when(step < t)
+        @pl.when(step < t // 2)
         def _():
-            out_ref[:, lanes] = jnp.zeros((TILE_R, TILE_C), jnp.float32)
-
-        @pl.when(step >= t)
+            out_ref[:, lanes] = jnp.zeros((tall, TILE_C), jnp.float32)
+
+        @pl.when(step >= t // 2)
         def _():
-            drop = (
-                dot_nt(hi_r, hi_c[lanes, :])
-                + dot_nt(hi_r, lo_c[lanes, :])
-                + dot_nt(lo_r, hi_c[lanes, :])
-            )
-            value = kernel_ref[:, lanes] - drop
+            all_c = jnp.concatenate([both_c[lanes, :], both_c[lanes, :PANEL]], axis=1)
+            value = kernel_ref[:, lanes] - dot_nt(all_r, all_c)
             if t == 0:
                 mine = left[col_index // 2]
                 mine = jnp.where(col_index % 2 == 1, pltpu.roll(mine, 64, 1), mine)
                 mine = jnp.concatenate([mine, mine], axis=1)
-                v = lax.broadcasted_iota(jnp.int32, (TILE_R, TILE_C), 1)
+                v = lax.broadcasted_iota(jnp.int32, (tall, TILE_C), 1)
                 value = jnp.where(v < 64, mine, value)
             out_ref[:, lanes] = value
 
-            @pl.when(step == t)
+            @pl.when(step == t // 2)
             def _():
-                out_ref[:, lanes] = masked(out_ref[:, lanes], t)
+                s = lax.broadcasted_iota(jnp.int32, (tall, TILE_C), 0)
+                v = lax.broadcasted_iota(jnp.int32, (tall, TILE_C), 1)
+                row_id = (step * 8 + s // 32) * PANEL + row_index * 32 + s % 32
+                col_id = (t * 4 + v // 64) * PANEL + col_index * 64 + v % 64
+                out_ref[:, lanes] = jnp.where(row_id >= col_id, out_ref[:, lanes], 0.0)
 
 
 def update(where, kernel, near, far, cols, v):
     n_rows, n_cols = kernel.shape
     piece = (1, TILE_R, PANEL)
+    halves = [
+        pl.BlockSpec(piece, lambda i, where, half=half: (slot_of(2 * i + half, where)[0], 0, 0))
+        for half in (0, 0, 1, 1)
+    ]
     return pl.pallas_call(
         update_kernel,
         out_shape=jax.ShapeDtypeStruct((n_rows, n_cols), jnp.float32),
         grid_spec=pltpu.PrefetchScalarGridSpec(
             num_scalar_prefetch=1,
-            grid=(n_rows // TILE_R,),
-            in_specs=[
-                pl.BlockSpec((TILE_R, n_cols), lambda i, where: (i, 0)),
-                pl.BlockSpec(piece, lambda i, where: (slot_of(i, where)[0], 0, 0)),
-                pl.BlockSpec(piece, lambda i, where: (slot_of(i, where)[0], 0, 0)),
+            grid=(n_rows // (2 * TILE_R),),
+            in_specs=[pl.BlockSpec((2 * TILE_R, n_cols), lambda i, where: (i, 0))]
+            + halves
+            + [
                 pl.BlockSpec((n_cols, PANEL), lambda i, where: (0, 0)),
                 pl.BlockSpec((PANEL, 2 * PANEL), lambda i, where: (0, 0)),
             ],
-            out_specs=pl.BlockSpec((TILE_R, n_cols), lambda i, where: (i, 0)),
+            out_specs=pl.BlockSpec((2 * TILE_R, n_cols), lambda i, where: (i, 0)),
             scratch_shapes=[
-                pltpu.VMEM((n_cols, PANEL), jnp.bfloat16),
-                pltpu.VMEM((n_cols, PANEL), jnp.bfloat16),
-                pltpu.VMEM((4, TILE_R, 128), jnp.float32),
+                pltpu.VMEM((n_cols, 2 * PANEL), jnp.bfloat16),
+                pltpu.VMEM((4, 2 * TILE_R, 128), jnp.float32),
             ],
         ),
         name="update",
         cost_estimate=pl.CostEstimate(flops=int(6e9), bytes_accessed=int(20e6), transcendentals=0),
-    )(where, kernel, near, far, cols, v)
+    )(where, kernel, near, far, near, far, cols, v)
 
 
 def send(x, target):
@@ -491,14 +490,8 @@
     return r, k ^ 1
 
 
-def to_columns(x):
-    moved = send(x, lambda r, k: (k * 2 + r % 2, r // 2))
-    return lax.all_gather(moved, "row", axis=0, tiled=True)
-
-
-def to_rows(x):
-    near = jnp.stack([x] + [send(x, along_z(d)) for d in (1, 2, 3)])
-    return near, send(near, other_core)
+def across(r, k):
+    return k * 2 + r % 2, r // 2
 
 
 def to_all(x):
@@ -511,22 +504,20 @@
 
 def per_device(samples):
     where = jnp.stack([lax.axis_index("row"), lax.axis_index("col")]).astype(jnp.int32)
-    pieces = to_all(samples)
-    if WAIT:
-        samples_later, pieces = lax.optimization_barrier((samples, pieces))
-    else:
-        samples_later = samples
+    row_feats = lax.all_gather(samples, "col", axis=0, tiled=True)
+    moved = send(samples, across)
+    moved, pieces = lax.optimization_barrier((moved, to_all(samples)))
+    col_feats = lax.all_gather(moved, "row", axis=0, tiled=True)
     corner, own = leading(where, pieces, samples)
-    col_feats = to_columns(samples_later)
-    own_cols = to_columns(own)
-    near_feats, far_feats = to_rows(samples_later)
-    near, far = to_rows(own)
+    moved = send(own, across)
+    shifted = [send(own, along_z(d)) for d in (1, 2, 3)]
     v = factor(corner)
-    kernel = tiles(where, near_feats, far_feats, col_feats)
+    moved, shifted, v = lax.optimization_barrier((moved, shifted, v))
+    own_cols = lax.all_gather(moved, "row", axis=0, tiled=True)
+    near = jnp.stack([own] + shifted)
+    far = send(near, other_core)
+    kernel = tiles(where, row_feats, col_feats)
     return update(where, kernel, near, far, own_cols, v)
-
-
-WAIT = True
 
 
 def solution(mesh):

time: 228 us -> 184 us (0.81)
  starting transfers between devices: 54 us -> 29.5 us
  Pallas kernels: 126 us -> 117 us
  waiting for transfers between devices: 28.5 us -> 20.9 us
    ppermute x19 -> x15, starting transfers between devices: 54 us -> 29.4 us  [send(): lax.ppermute(x, ('row', 'col'), [(s, t[0] * 8 + t[1]) for s, t in pairs i...]
    ppermute x19 -> x15, waiting for transfers between devices: 28.4 us -> 13.8 us  [send(): lax.ppermute(x, ('row', 'col'), [(s, t[0] * 8 + t[1]) for s, t in pairs i...]
    pallas_call x1, Pallas kernels: 29.3 us -> 20.8 us  [update(): pl.pallas_call(update_kernel, out_shape=jax.ShapeDtypeStruct((n_rows, n_c...]
    all_gather x2 -> x3, waiting for transfers between devices: 0.02 us -> 6.29 us  [the longest x1 6.25 us: per_device(): own_cols = lax.all_gather(moved, 'row', axis=0, tiled=True)]
  transfers between devices with their start and end apart: 21 -> 18, of which waited for: 13 -> 7; matrix products, arithmetic and copies ran while one was open for 0% -> 1% of each run, Pallas kernels for 43% -> 52%
where the time goes in v3:
time: 184 us; the launch traced here: 183 us
  Pallas kernels  117 us (64%)
  starting transfers between devices  29.5 us (16%)
  waiting for transfers between devices  20.9 us (11%)
  between operations  13.3 us (7%)
  other arithmetic  2.33 us (1%)
    pallas_call x1, Pallas kernels, tiles(): pl.pallas_call(tiles_kernel, out_shape=jax.ShapeDtypeStruct((n_rows, n_co...  45.8 us
    pallas_call x1, Pallas kernels, factor(): pl.pallas_call(factor_kernel, out_shape=jax.ShapeDtypeStruct((PANEL, 2 *...  38.6 us
    ppermute x15, starting transfers between devices, send(): lax.ppermute(x, ('row', 'col'), [(s, t[0] * 8 + t[1]) for s, t in pairs i...  29.4 us
    pallas_call x1, Pallas kernels, update(): pl.pallas_call(update_kernel, out_shape=jax.ShapeDtypeStruct((n_rows, n_c...  20.8 us
    ppermute x15, waiting for transfers between devices, send(): lax.ppermute(x, ('row', 'col'), [(s, t[0] * 8 + t[1]) for s, t in pairs i...  13.8 us
    pallas_call x1, Pallas kernels, leading(): pl.pallas_call(leading_kernel, out_shape=(jax.ShapeDtypeStruct((PANEL, PA...  11.6 us
    all_gather x1, waiting for transfers between devices, per_device(): own_cols = lax.all_gather(moved, 'row', axis=0, tiled=True)  6.25 us
  transfers between devices with their start and end apart: 18, of which 7 were waited for; matrix products, arithmetic and copies ran while one was open for 1% of the time, Pallas kernels for 52%

profile of v3, /device:TPU:1, one launch (start us, length us, event | category | flops | bytes accessed | tf_op | source)
XLA Modules:
  0.0 183.5 jit_solution(1994996024657023878)
XLA Ops:
  6.5 0.7 all-gather.4.cloned.1.call-update
  7.3 0.8 slice_select_fusion
  8.1 1.3 collective-permute-start.1
  9.4 2.1 %collective-permute-done.1 = bf16[32,768]{1,0:T(8,128)(2,1)S(1)} collective-permute-done((bf16[32,768]{1,0:T(8,128)(2,1)S(1)}, bf16[32,768]{1,0:T(8,128)(2,1)S(1)}, u32[]{:S(2)}, u32[]{:S(2)}) %collective-permute-start.1) | collective-permute-done | bytes 49184 | tf_op jit(solution)/shard_map/ppermute | solution.py:474
  11.5 0.8 fusion
  12.3 1.7 collective-permute-start.2
  14.0 1.2 collective-permute-done.2
  15.1 1.5 collective-permute-start.3
  16.6 1.2 collective-permute-done.3
  17.8 2.8 %collective-permute-start.6 = (bf16[32,768]{1,0:T(8,128)(2,1)S(1)}, bf16[32,768]{1,0:T(8,128)(2,1)S(1)}, u32[]{:S(2)}, u32[]{:S(2)}) collective-permute-start(bf16[32,768]{1,0:T(8,128)(2,1)S(1)} %add.11), channel_id=1, source_target_pairs={{0,96},{1,97},{2,98},{3,99},{4,100},{5,101},{6,102},{7,103},{8,104... | collective-permute-start | bytes 147464 | tf_op jit(solution)/shard_map/ppermute | solution.py:474
  21.6 7.3 %collective-permute-start = (bf16[128,768]{1,0:T(8,128)(2,1)}, bf16[128,768]{1,0:T(8,128)(2,1)S(1)}, u32[]{:S(2)}, u32[]{:S(2)}) collective-permute-start(bf16[128,768]{1,0:T(8,128)(2,1)} %own_ref.1), channel_id=1, source_target_pairs={{0,0},{1,16},{2,32},{3,48},{4,64},{5,80},{6,96},{7,112},{8,8},{9,2... | collective-permute-start | bytes 589832 | tf_op jit(solution)/shard_map/ppermute | solution.py:474
  29.1 2.1 %collective-permute-start.8 = (bf16[4,32,768]{2,1,0:T(8,128)(2,1)S(1)}, bf16[4,32,768]{2,1,0:T(8,128)(2,1)S(1)}, u32[]{:S(2)}, u32[]{:S(2)}) collective-permute-start(bf16[4,32,768]{2,1,0:T(8,128)(2,1)S(1)} %pad_maximum_fusion.1.g0), channel_id=1, source_target_pairs={{0,16},{1,17},{2,18},{3,19},{4,20},{5,21},{6,22},{7,23},{8,24},{9,... | collective-permute-start | bytes 589832 | tf_op jit(solution)/shard_map/ppermute | solution.py:474
  31.2 1.4 collective-permute-done
  32.5 5.1 %collective-permute-done.9.g3 = bf16[4,32,768]{2,1,0:T(8,128)(2,1)S(1)} collective-permute-done((bf16[4,32,768]{2,1,0:T(8,128)(2,1)S(1)}, bf16[4,32,768]{2,1,0:T(8,128)(2,1)S(1)}, u32[]{:S(2)}, u32[]{:S(2)}) %collective-permute-start.9) | collective-permute-done | bytes 196640 | tf_op jit(solution)/shard_map/ppermute | solution.py:474
  37.7 2.9 %collective-permute-done.7.g1 = bf16[4,32,768]{2,1,0:T(8,128)(2,1)S(1)} collective-permute-done((bf16[4,32,768]{2,1,0:T(8,128)(2,1)S(1)}, bf16[4,32,768]{2,1,0:T(8,128)(2,1)S(1)}, u32[]{:S(2)}, u32[]{:S(2)}) %collective-permute-start.7) | collective-permute-done | bytes 196640 | tf_op jit(solution)/shard_map/ppermute | solution.py:474
  41.3 11.6 %leading.1 = (f32[512,512]{1,0:T(8,128)}, f32[128,512]{1,0:T(8,128)}) custom-call(s32[2]{0:T(128)} %pad_add_fusion.where_ref, bf16[4,32,768]{2,1,0:T(8,128)(2,1)} %copy-done.5, bf16[4,32,768]{2,1,0:T(8,128)(2,1)} %copy-done.8, bf16[4,32,768]{2,1,0:T(8,128)(2,1)} %copy-done.7, bf16[4,32,768]{2,1,0:T(8,128)(2,1)} %copy-done.6, bf16[128,768]{1,0:T(8,128)(2,1)} %own_ref.1), custom_call_target="tpu_custom_call" | custom-call | flops 8000000000 | bytes 2000000 | tf_op jit(solution)/shard_map/leading/pallas_call | solution.py:165
  52.8 3.7 %collective-permute-start.13 = (f32[128,512]{1,0:T(8,128)}, f32[128,512]{1,0:T(8,128)S(1)}, u32[]{:S(2)}, u32[]{:S(2)}) collective-permute-start(f32[128,512]{1,0:T(8,128)} %get-tuple-element.22), channel_id=1, source_target_pairs={{0,6},{1,7},{2,0},{3,1},{4,2},{5,3},{6,4},{7,5},{8,14},{9,15},{10,... | collective-permute-start | bytes 786440 | tf_op jit(solution)/shard_map/ppermute | solution.py:474
  56.6 1.0 collective-permute-start.12
  58.3 6.0 %collective-permute-start.10 = (f32[128,512]{1,0:T(8,128)}, f32[128,512]{1,0:T(8,128)S(1)}, u32[]{:S(2)}, u32[]{:S(2)}) collective-permute-start(f32[128,512]{1,0:T(8,128)} %get-tuple-element.22), channel_id=1, source_target_pairs={{0,0},{1,16},{2,32},{3,48},{4,64},{5,80},{6,96},{7,112},{8,8},{9,2... | collective-permute-start | bytes 786440 | tf_op jit(solution)/shard_map/ppermute | solution.py:474
  64.3 38.6 %factor.1.refs_5_ = bf16[512,1024]{1,0:T(8,128)(2,1)} custom-call(f32[512,512]{1,0:T(8,128)} %get-tuple-element.23.corner_ref), custom_call_target="tpu_custom_call" | custom-call | flops 24999999488 | bytes 2000000 | tf_op jit(solution)/shard_map/factor/pallas_call | solution.py:260
  102.9 0.7 copy-done.2
  104.1 45.8 %tiles.1.kernel_ref = f32[1024,2048]{1,0:T(8,128)} custom-call(s32[2]{0:T(128)} %pad_add_fusion.where_ref, bf16[1024,768]{1,0:T(8,128)(2,1)} %all-gather.4.cloned.1.call-done.rows_ref, bf16[2048,768]{1,0:T(8,128)(2,1)} %all-gather.6.cloned.1.call-done.cols_ref), custom_call_target="tpu_custom_call" | custom-call | flops 30000001024 | bytes 12000000 | tf_op jit(solution)/shard_map/tiles/pallas_call | solution.py:347
  149.9 6.3 %all-gather.8.cloned.1.call-done.refs_4_ = f32[2048,512]{1,0:T(8,128)} async-done(((f32[128,512]{1,0:T(8,128)}), f32[2048,512]{1,0:T(8,128)}) %all-gather.8.cloned.1.call-update) | async-done | bytes 4194320 | tf_op jit(solution)/shard_map/all_gather | solution.py:516
  156.1 20.8 %update.1 = f32[1024,2048]{1,0:T(8,128)} custom-call(s32[2]{0:T(128)} %pad_add_fusion.where_ref, f32[1024,2048]{1,0:T(8,128)} %tiles.1.kernel_ref, f32[4,128,512]{2,1,0:T(8,128)} %copy-done, f32[4,128,512]{2,1,0:T(8,128)} %copy-done.1, f32[4,128,512]{2,1,0:T(8,128)} %copy-done, f32[4,128,512]{2,1,0:T(8,128)} %copy-done.1, ...), custom_call_target="tpu_custom_call" | custom-call | flops 6000000000 | bytes 20000000 | tf_op jit(solution)/shard_map/update/pallas_call | solution.py:449
  (44 shorter events, 3.0 us)
Async XLA Ops:
  6.5 97.5 %all-gather.4.cloned.1.call-start = ((), (), s32[]{:S(2)}) async-start(), calls=%async_computation | async-start | bytes 1769472 | tf_op jit(solution)/shard_map/all_gather | solution.py:507
  7.3 96.8 %all-gather.6.cloned.1.call-start = ((), (), s32[]{:S(2)}) async-start(), calls=%async_computation.1 | async-start | bytes 3342336 | tf_op jit(solution)/shard_map/all_gather | solution.py:510
  8.1 3.4 %collective-permute-start.1 = (bf16[32,768]{1,0:T(8,128)(2,1)S(1)}, bf16[32,768]{1,0:T(8,128)(2,1)S(1)}, u32[]{:S(2)}, u32[]{:S(2)}) collective-permute-start(bf16[32,768]{1,0:T(8,128)(2,1)S(1)} %slice_select_fusion), channel_id=1, source_target_pairs={{0,1},{8,9},{16,17},{24,25},{32,33},{40,41},{48,49},{56,57},{64,65... | collective-permute-start | bytes 147464 | tf_op jit(solution)/shard_map/ppermute | solution.py:474
  12.3 2.8 %collective-permute-start.2 = (bf16[32,768]{1,0:T(8,128)(2,1)S(1)}, bf16[32,768]{1,0:T(8,128)(2,1)S(1)}, u32[]{:S(2)}, u32[]{:S(2)}) collective-permute-start(bf16[32,768]{1,0:T(8,128)(2,1)S(1)} %fusion), channel_id=1, source_target_pairs={{0,2},{1,3},{8,10},{9,11},{16,18},{17,19},{24,26},{25,27},{32,34},... | collective-permute-start | bytes 147464 | tf_op jit(solution)/shard_map/ppermute | solution.py:474
  15.1 2.6 %collective-permute-start.3 = (bf16[32,768]{1,0:T(8,128)(2,1)S(1)}, bf16[32,768]{1,0:T(8,128)(2,1)S(1)}, u32[]{:S(2)}, u32[]{:S(2)}) collective-permute-start(bf16[32,768]{1,0:T(8,128)(2,1)S(1)} %add.10), channel_id=1, source_target_pairs={{0,4},{1,5},{2,6},{3,7},{8,12},{9,13},{10,14},{11,15},{16,20},{17,... | collective-permute-start | bytes 147464 | tf_op jit(solution)/shard_map/ppermute | solution.py:474
  17.8 11.1 %collective-permute-start.6 = (bf16[32,768]{1,0:T(8,128)(2,1)S(1)}, bf16[32,768]{1,0:T(8,128)(2,1)S(1)}, u32[]{:S(2)}, u32[]{:S(2)}) collective-permute-start(bf16[32,768]{1,0:T(8,128)(2,1)S(1)} %add.11), channel_id=1, source_target_pairs={{0,96},{1,97},{2,98},{3,99},{4,100},{5,101},{6,102},{7,103},{8,104... | collective-permute-start | bytes 147464 | tf_op jit(solution)/shard_map/ppermute | solution.py:474
  20.6 8.3 %collective-permute-start.5 = (bf16[32,768]{1,0:T(8,128)(2,1)S(1)}, bf16[32,768]{1,0:T(8,128)(2,1)S(1)}, u32[]{:S(2)}, u32[]{:S(2)}) collective-permute-start(bf16[32,768]{1,0:T(8,128)(2,1)S(1)} %add.11), channel_id=1, source_target_pairs={{0,64},{1,65},{2,66},{3,67},{4,68},{5,69},{6,70},{7,71},{8,72},{9,... | collective-permute-start | bytes 147464 | tf_op jit(solution)/shard_map/ppermute | solution.py:474
  21.0 8.0 %collective-permute-start.4 = (bf16[32,768]{1,0:T(8,128)(2,1)S(1)}, bf16[32,768]{1,0:T(8,128)(2,1)S(1)}, u32[]{:S(2)}, u32[]{:S(2)}) collective-permute-start(bf16[32,768]{1,0:T(8,128)(2,1)S(1)} %add.11), channel_id=1, source_target_pairs={{0,32},{1,33},{2,34},{3,35},{4,36},{5,37},{6,38},{7,39},{8,40},{9,... | collective-permute-start | bytes 147464 | tf_op jit(solution)/shard_map/ppermute | solution.py:474
  21.6 10.9 %collective-permute-start = (bf16[128,768]{1,0:T(8,128)(2,1)}, bf16[128,768]{1,0:T(8,128)(2,1)S(1)}, u32[]{:S(2)}, u32[]{:S(2)}) collective-permute-start(bf16[128,768]{1,0:T(8,128)(2,1)} %own_ref.1), channel_id=1, source_target_pairs={{0,0},{1,16},{2,32},{3,48},{4,64},{5,80},{6,96},{7,112},{8,8},{9,2... | collective-permute-start | bytes 589832 | tf_op jit(solution)/shard_map/ppermute | solution.py:474
  29.0 12.3 %copy-start.5 = (bf16[4,32,768]{2,1,0:T(8,128)(2,1)}, bf16[4,32,768]{2,1,0:T(8,128)(2,1)S(1)}, u32[]{:S(2)}) copy-start(bf16[4,32,768]{2,1,0:T(8,128)(2,1)S(1)} %pad_maximum_fusion.1.g0) | copy-start | bytes 589828
  29.0 8.7 %collective-permute-start.9 = (bf16[4,32,768]{2,1,0:T(8,128)(2,1)S(1)}, bf16[4,32,768]{2,1,0:T(8,128)(2,1)S(1)}, u32[]{:S(2)}, u32[]{:S(2)}) collective-permute-start(bf16[4,32,768]{2,1,0:T(8,128)(2,1)S(1)} %pad_maximum_fusion.1.g0), channel_id=1, source_target_pairs={{0,24},{1,25},{2,26},{3,27},{4,28},{5,29},{6,30},{7,31},{8,0},{9,1... | collective-permute-start | bytes 589832 | tf_op jit(solution)/shard_map/ppermute | solution.py:474
  29.1 8.6 %collective-permute-start.8 = (bf16[4,32,768]{2,1,0:T(8,128)(2,1)S(1)}, bf16[4,32,768]{2,1,0:T(8,128)(2,1)S(1)}, u32[]{:S(2)}, u32[]{:S(2)}) collective-permute-start(bf16[4,32,768]{2,1,0:T(8,128)(2,1)S(1)} %pad_maximum_fusion.1.g0), channel_id=1, source_target_pairs={{0,16},{1,17},{2,18},{3,19},{4,20},{5,21},{6,22},{7,23},{8,24},{9,... | collective-permute-start | bytes 589832 | tf_op jit(solution)/shard_map/ppermute | solution.py:474
  31.2 9.4 %collective-permute-start.7 = (bf16[4,32,768]{2,1,0:T(8,128)(2,1)S(1)}, bf16[4,32,768]{2,1,0:T(8,128)(2,1)S(1)}, u32[]{:S(2)}, u32[]{:S(2)}) collective-permute-start(bf16[4,32,768]{2,1,0:T(8,128)(2,1)S(1)} %pad_maximum_fusion.1.g0), channel_id=1, source_target_pairs={{0,8},{1,9},{2,10},{3,11},{4,12},{5,13},{6,14},{7,15},{8,16},{9,17... | collective-permute-start | bytes 589832 | tf_op jit(solution)/shard_map/ppermute | solution.py:474
  32.5 8.1 %copy-start.4 = (bf16[128,768]{1,0:T(8,128)(2,1)}, bf16[128,768]{1,0:T(8,128)(2,1)S(1)}, u32[]{:S(2)}) copy-start(bf16[128,768]{1,0:T(8,128)(2,1)S(1)} %collective-permute-done) | copy-start | bytes 589828
  37.7 3.6 %copy-start.6 = (bf16[4,32,768]{2,1,0:T(8,128)(2,1)}, bf16[4,32,768]{2,1,0:T(8,128)(2,1)S(1)}, u32[]{:S(2)}) copy-start(bf16[4,32,768]{2,1,0:T(8,128)(2,1)S(1)} %collective-permute-done.9.g3) | copy-start | bytes 589828
  40.6 115.5 %all-gather.8.cloned.1.call-start = ((), (), s32[]{:S(2)}) async-start(), calls=%async_computation.2 | async-start | bytes 4456448 | tf_op jit(solution)/shard_map/all_gather | solution.py:516
  52.8 50.0 %collective-permute-start.13 = (f32[128,512]{1,0:T(8,128)}, f32[128,512]{1,0:T(8,128)S(1)}, u32[]{:S(2)}, u32[]{:S(2)}) collective-permute-start(f32[128,512]{1,0:T(8,128)} %get-tuple-element.22), channel_id=1, source_target_pairs={{0,6},{1,7},{2,0},{3,1},{4,2},{5,3},{6,4},{7,5},{8,14},{9,15},{10,... | collective-permute-start | bytes 786440 | tf_op jit(solution)/shard_map/ppermute | solution.py:474
  56.6 46.3 %collective-permute-start.12 = (f32[128,512]{1,0:T(8,128)}, f32[128,512]{1,0:T(8,128)S(1)}, u32[]{:S(2)}, u32[]{:S(2)}) collective-permute-start(f32[128,512]{1,0:T(8,128)} %get-tuple-element.22), channel_id=1, source_target_pairs={{0,4},{1,5},{2,6},{3,7},{4,0},{5,1},{6,2},{7,3},{8,12},{9,13},{10,... | collective-permute-start | bytes 786440 | tf_op jit(solution)/shard_map/ppermute | solution.py:474
  57.6 45.3 %collective-permute-start.11 = (f32[128,512]{1,0:T(8,128)}, f32[128,512]{1,0:T(8,128)S(1)}, u32[]{:S(2)}, u32[]{:S(2)}) collective-permute-start(f32[128,512]{1,0:T(8,128)} %get-tuple-element.22), channel_id=1, source_target_pairs={{0,2},{1,3},{2,4},{3,5},{4,6},{5,7},{6,0},{7,1},{8,10},{9,11},{10,... | collective-permute-start | bytes 786440 | tf_op jit(solution)/shard_map/ppermute | solution.py:474
  58.3 44.6 %collective-permute-start.10 = (f32[128,512]{1,0:T(8,128)}, f32[128,512]{1,0:T(8,128)S(1)}, u32[]{:S(2)}, u32[]{:S(2)}) collective-permute-start(f32[128,512]{1,0:T(8,128)} %get-tuple-element.22), channel_id=1, source_target_pairs={{0,0},{1,16},{2,32},{3,48},{4,64},{5,80},{6,96},{7,112},{8,8},{9,2... | collective-permute-start | bytes 786440 | tf_op jit(solution)/shard_map/ppermute | solution.py:474
  64.2 39.4 %copy-start.3 = (f32[128,512]{1,0:T(8,128)S(1)}, f32[128,512]{1,0:T(8,128)}, u32[]{:S(2)}) copy-start(f32[128,512]{1,0:T(8,128)} %get-tuple-element.22) | copy-start | bytes 786436
  103.7 46.2 %copy-start = (f32[4,128,512]{2,1,0:T(8,128)}, f32[4,128,512]{2,1,0:T(8,128)S(1)}, u32[]{:S(2)}) copy-start(f32[4,128,512]{2,1,0:T(8,128)S(1)} %pad_maximum_fusion.refs_0_.refs_2_) | copy-start | bytes 3145732
  103.7 46.2 %collective-permute-start.14 = (f32[4,128,512]{2,1,0:T(8,128)S(1)}, f32[4,128,512]{2,1,0:T(8,128)S(1)}, u32[]{:S(2)}, u32[]{:S(2)}) collective-permute-start(f32[4,128,512]{2,1,0:T(8,128)S(1)} %pad_maximum_fusion.refs_0_.refs_2_), channel_id=1, source_target_pairs={{0,1},{1,0},{2,3},{3,2},{4,5},{5,4},{6,7},{7,6},{8,9},{9,8},{10,11... | collective-permute-start | bytes 3145736 | tf_op jit(solution)/shard_map/ppermute | solution.py:474
  149.9 6.3 %copy-start.1 = (f32[4,128,512]{2,1,0:T(8,128)}, f32[4,128,512]{2,1,0:T(8,128)S(1)}, u32[]{:S(2)}) copy-start(f32[4,128,512]{2,1,0:T(8,128)S(1)} %collective-permute-done.14.refs_1_.refs_3_) | copy-start | bytes 3145732
  (3 other events, 5.0 us)
Sparse Core Ops, SparseCore 0:
  9.0 30.8 all-gather.3
  42.0 57.8 all-gather.5
  103.7 52.3 all-gather.7
